TPU v7x, 512 devices: a whole 4x4x16 slice. The times are simulated.
512 devices in a mesh: section: 32 (over z, x_hi), dp: 4 (over y), mp: 4 (over x_lo, core).
Axes of the slice: x: 4 (x_hi: 2, x_lo: 2; x = x_hi * 2 + x_lo), y: 4, z: 16, core: 2. Of those that a mesh axis runs over, the one named last changes fastest.
Arguments:
- memory: bfloat16 [4, 256, 2048], P('dp', None, ('section', 'mp')), may hold values from -18 to 18
- key_weight: bfloat16 [32, 2048, 2048], P('section', None, 'mp'), may hold values from -1 to 1
- value_weight: bfloat16 [32, 2048, 2048], P('section', None, 'mp'), may hold values from -0.125 to 0.125
- queries: bfloat16 [32, 4, 256, 2048], P('section', 'dp', None, 'mp'), may hold values from -1024 to 1024
- cotangent: bfloat16 [32, 4, 256, 2048], P('section', 'dp', None, 'mp'), may hold values from -6 to 6
- target_lengths: int32 [4], P('dp'), may hold values from 64 to 256, as said below
Outputs:
- context: bfloat16 [32, 4, 256, 2048], P('section', 'dp', None, 'mp')
- mem_grad: float32 [4, 256, 2048], P('dp', None, ('section', 'mp'))
Inputs may be any that keep to these rules, and one draw needn't show every extreme that they name: `target_lengths`: valid positions of a sequence come first; the last sequence is full.
All inputs are finite; a program needn't handle non-finite values.
Results may differ from a plain program's by a relative error of at most 0.013.
The roundings to bfloat16 on the way count: a program that leaves them out, or rounds other values in their place, can miss the bound.
Values may be sent and summed in bfloat16 or wider, within the bound.
No kernel may reach another device: no remote copies, remote signals or barrier semaphores. Data moves between devices by JAX's collectives and lax.ppermute only.
A program may use at most 64 MiB of HBM per device.

v0:
```python
import jax
import jax.numpy as jnp
from jax import lax
from jax.sharding import PartitionSpec as P

HEAD_DIM = 256


def on_device(memory, key_weight, value_weight, queries, cotangent, target_lengths):
    width = key_weight.shape[2]
    head_count = width // HEAD_DIM
    seq_rows = queries.shape[2]
    score_scale = HEAD_DIM ** (-0.5)
    mem_block = memory[0]
    mem_rows = mem_block.shape[0]
    full_memory = lax.all_gather(mem_block, ("section", "mp"), axis=1, tiled=True)
    token_total = lax.psum(target_lengths.astype(jnp.float32), "dp")
    slot_total = float(lax.axis_size("dp") * target_lengths.shape[0] * seq_rows)
    loss_weight = slot_total / token_total[0]
    valid = (jnp.arange(seq_rows, dtype=jnp.int32) < target_lengths[0]).astype(jnp.float32)
    layer_index = 0
    key_rows = jnp.dot(
        full_memory, key_weight[layer_index], preferred_element_type=jnp.float32
    ).astype(jnp.bfloat16)
    value_rows = jnp.dot(
        full_memory, value_weight[layer_index], preferred_element_type=jnp.float32
    ).astype(jnp.bfloat16)
    key_heads = key_rows.reshape(mem_rows, head_count, HEAD_DIM)
    value_heads = value_rows.reshape(mem_rows, head_count, HEAD_DIM)
    query_heads = queries[layer_index, 0].reshape(seq_rows, head_count, HEAD_DIM)
    scores = (
        jnp.einsum("thd,shd->hts", query_heads, key_heads, preferred_element_type=jnp.float32)
        * score_scale
    )
    attention = jax.nn.softmax(scores, axis=-1)
    attention_low = attention.astype(jnp.bfloat16)
    context = jnp.einsum(
        "hts,shd->thd", attention_low, value_heads, preferred_element_type=jnp.float32
    )
    context = (context * valid[:, None, None]).astype(jnp.bfloat16)
    contexts = [context.reshape(seq_rows, width)]
    weighted = cotangent[layer_index, 0].astype(jnp.float32) * (valid * loss_weight)[:, None]
    weighted = weighted.astype(jnp.bfloat16).reshape(seq_rows, head_count, HEAD_DIM)
    value_grad = jnp.einsum(
        "hts,thd->shd", attention_low, weighted, preferred_element_type=jnp.float32
    )
    value_grads = [value_grad.astype(jnp.bfloat16).reshape(mem_rows, width)]
    prob_grad = jnp.einsum(
        "thd,shd->hts", weighted, value_heads, preferred_element_type=jnp.float32
    )
    row_dot = jnp.sum(attention * prob_grad, axis=-1, keepdims=True)
    score_grad = (attention * (prob_grad - row_dot) * score_scale).astype(jnp.bfloat16)
    key_grad = jnp.einsum(
        "hts,thd->shd", score_grad, query_heads, preferred_element_type=jnp.float32
    )
    key_grads = [key_grad.astype(jnp.bfloat16).reshape(mem_rows, width)]
    contract_last = (((1,), (1,)), ((), ()))
    layer_index = 0
    key_part = key_weight[layer_index]
    value_part = value_weight[layer_index]
    running = lax.dot_general(
        key_part, key_grads[layer_index], contract_last, preferred_element_type=jnp.float32
    )
    running = running + lax.dot_general(
        value_part, value_grads[layer_index], contract_last, preferred_element_type=jnp.float32
    )
    own_part = lax.psum_scatter(running, ("section", "mp"), scatter_dimension=0, tiled=True)
    own_grad = own_part.T
    context_out = jnp.stack(contexts, axis=0)[:, None]
    return (context_out, own_grad[None])


def solution(mesh):
    return jax.shard_map(
        on_device,
        mesh=mesh,
        in_specs=(
            P("dp", None, ("section", "mp")),
            P("section", None, "mp"),
            P("section", None, "mp"),
            P("section", "dp", None, "mp"),
            P("section", "dp", None, "mp"),
            P("dp"),
        ),
        out_specs=(P("section", "dp", None, "mp"), P("dp", None, ("section", "mp"))),
        check_vma=False,
    )
```

profile of v0, /device:TPU:8, one launch (start us, length us, event | category | flops | bytes accessed | tf_op | source)
XLA Modules:
  0.0 430.5 jit_solution(5405295528852739863)
XLA Ops:
  7.2 0.0 copy-start
  7.2 0.0 all-gather.3.cloned.1.call-start
  7.2 0.7 all-gather.3.cloned.1.call-update
  7.9 0.0 reduce-scatter.4.cloned.1.call-start
  8.6 14.0 %psum.7 = f32[1]{0:T(128)} all-reduce(f32[1]{0:T(128)S(6)} %convert_element_type.59), channel_id=1, replica_groups=mesh['section'=32,'dp'=4,'mp'=4] {'dp'}, use_global_device_ids=true, to_apply=%region_2.0 | all-reduce | flops 1 | bytes 8 | tf_op jit(solution)/shard_map/psum | solution.py:17
  22.6 1.1 copy.41
  23.7 1.2 copy.38
  25.6 120.8 %all-gather.3.cloned.1.call-done = bf16[1,256,2048]{1,2,0:T(8,128)(2,1)} async-done(((bf16[1,256,16]{1,2,0:T(8,128)(2,1)}), bf16[1,256,2048]{1,2,0:T(8,128)(2,1)}) %all-gather.3.cloned.1.call-update) | async-done | bytes 1048592 | tf_op jit(solution)/shard_map/all_gather | solution.py:16
  146.4 0.0 copy-done
  146.4 1.9 fusion.22
  148.4 0.0 copy-start.6
  148.4 0.0 copy-done.2
  148.4 1.1 fusion.58
  149.5 2.6 fusion.19
  152.2 0.0 copy-start.4
  152.2 0.2 fusion.33
  152.4 0.5 copy-done.4
  152.9 1.6 convolution_convert_fusion
  154.5 1.6 fusion.18
  156.1 0.0 copy-start.1
  156.1 0.8 fusion.3
  156.9 0.8 copy-done.1
  157.7 2.1 fusion.2
  159.8 2.9 copy.39
  162.8 0.0 reduce-scatter.4.cloned.1.call-update
  162.8 0.9 copy-done.3
  163.7 0.1 copy-done.5
  163.8 1.5 fusion.25
  165.3 0.8 copy.32
  166.2 256.0 %reduce-scatter.4.cloned.1.call-done = f32[16,256]{1,0:T(8,128)} async-done(((f32[2048,256]{1,0:T(8,128)}), f32[16,256]{1,0:T(8,128)}) %reduce-scatter.4.cloned.1.call-update) | async-done | bytes 16400
  422.2 0.8 copy.40
  423.0 0.7 copy.33
  (6 shorter events, 0.0 us)
Async XLA Ops:
  7.2 139.3 %copy-start = (bf16[1,2048,512]{2,1,0:T(8,128)(2,1)S(1)}, bf16[1,2048,512]{2,1,0:T(8,128)(2,1)}, u32[]{:S(2)}) copy-start(bf16[1,2048,512]{2,1,0:T(8,128)(2,1)} %param.7) | copy-start | bytes 6291460
  7.2 139.2 %all-gather.3.cloned.1.call-start = ((), (), s32[]{:S(2)}) async-start(), calls=%async_computation.1 | async-start | bytes 1056768 | tf_op jit(solution)/shard_map/all_gather | solution.py:16
  7.9 414.3 %reduce-scatter.4.cloned.1.call-start = ((), (), s32[]{:S(2)}) async-start(), calls=%async_computation.2 | async-start | bytes 2113536
  23.7 124.7 %copy-start.2 = (bf16[1,1,256,512]{2,3,1,0:T(8,128)(2,1)}, bf16[1,1,256,512]{2,3,1,0:T(8,128)(2,1)S(1)}, u32[]{:S(2)}) copy-start(bf16[1,1,256,512]{2,3,1,0:T(8,128)(2,1)S(1)} %copy.41) | copy-start | bytes 786436
  148.4 3.8 copy-start.6
  152.2 0.7 copy-start.4
  156.1 1.6 copy-start.1
  162.7 0.9 copy-start.3
  162.8 1.0 copy-start.5
Sparse Core Ops, SparseCore 0:
  11.0 135.4 all-gather.2
  162.9 259.2 reduce-scatter.3
where the time goes:
time: 431 us
  waiting for transfers between devices  378 us (88%)
  between operations  15.5 us (4%)
  blocking collectives  14 us (3%)
  matrix products  13.5 us (3%)
  local copies, waits for them, and re-layouts  9.84 us (2%)
    unnamed x3, waiting for transfers between devices  257 us
    all_gather x1, waiting for transfers between devices, on_device(): lax.all_gather(mem_block, ('section', 'mp'), axis=1, tiled=True)  121 us
    psum x1, blocking collectives, on_device(): token_total = lax.psum(target_lengths.astype(jnp.float32), 'dp')  14 us
  transfers between devices with their start and end apart: 2, of which 2 were waited for; matrix products, arithmetic and copies ran while one was open for 1% of the time, Pallas kernels for 0%

commit v1 on v0

v1 whole, which is shorter than its diff:
```python
import jax
import jax.numpy as jnp
from jax import lax
from jax.experimental import pallas as pl
from jax.experimental.pallas import tpu as pltpu
from jax.sharding import Mesh, PartitionSpec as P

HEAD_DIM = 256
NT = (((1,), (1,)), ((), ()))
TN = (((0,), (0,)), ((), ()))
X = ("xh", "xl")


def dot(a, b, dims=(((1,), (0,)), ((), ()))):
    return lax.dot_general(a, b, dims, preferred_element_type=jnp.float32)


def local_kernel(
    core_ref, length_ref, own_ref, other_ref, wk_ref, wv_ref, q_ref, cot_ref,
    context_ref, keep_ref, send_ref, mt_ref, m_ref, kg_ref, vg_ref,
):
    core = core_ref[0]
    length = length_ref[0]
    n_x, n_z, blk, rows = own_ref.shape
    span = n_x * blk * 2
    width = wk_ref.shape[1]
    scale = HEAD_DIM ** (-0.5)
    for z in range(n_z):
        for x in range(n_x):
            base = z * span + x * 2 * blk
            mt_ref[pl.ds(pl.multiple_of(base + core * blk, blk), blk), :] = own_ref[x, z]
            mt_ref[pl.ds(pl.multiple_of(base + (1 - core) * blk, blk), blk), :] = other_ref[x, z]
    for z in range(n_z):
        m_ref[:, z * span:(z + 1) * span] = mt_ref[z * span:(z + 1) * span, :].T
    keys = dot(m_ref[...], wk_ref[...]).astype(jnp.bfloat16)
    values = dot(m_ref[...], wv_ref[...]).astype(jnp.bfloat16)
    t_rows = q_ref.shape[0]
    valid = lax.broadcasted_iota(jnp.int32, (t_rows, HEAD_DIM), 0) < length
    for h in range(width // HEAD_DIM):
        cols = slice(h * HEAD_DIM, (h + 1) * HEAD_DIM)
        key, value, query = keys[:, cols], values[:, cols], q_ref[:, cols]
        scores = dot(key, query, NT) * scale
        weights = jnp.exp(scores - jnp.max(scores, axis=0, keepdims=True))
        probs = weights / jnp.sum(weights, axis=0, keepdims=True)
        probs_low = probs.astype(jnp.bfloat16)
        context = dot(probs_low, value, TN)
        context_ref[:, cols] = jnp.where(valid, context, 0.0).astype(jnp.bfloat16)
        cot = jnp.where(valid, cot_ref[:, cols].astype(jnp.float32), 0.0).astype(jnp.bfloat16)
        vg_ref[:, cols] = dot(probs_low, cot).astype(jnp.bfloat16)
        prob_grad = dot(value, cot, NT)
        row_dot = jnp.sum(probs * prob_grad, axis=0, keepdims=True)
        score_grad = (probs * (prob_grad - row_dot) * scale).astype(jnp.bfloat16)
        kg_ref[:, cols] = dot(score_grad, query).astype(jnp.bfloat16)
    first = core == 0
    for z in range(0, n_z, 2):
        at = slice(z * span, (z + 2) * span)
        grad = dot(wk_ref[at, :], kg_ref[...], NT) + dot(wv_ref[at, :], vg_ref[...], NT)
        for dz in range(2):
            for x in range(n_x):
                lo = dz * span + x * 2 * blk
                g0, g1 = grad[lo:lo + blk], grad[lo + blk:lo + 2 * blk]
                keep_ref[x, z + dz] = jnp.where(first, g0, g1).astype(jnp.bfloat16)
                send_ref[x, z + dz] = jnp.where(first, g1, g0).astype(jnp.bfloat16)


def on_device(memory, key_weight, value_weight, queries, cotangent, target_lengths):
    n_z, n_x = lax.axis_size("z"), lax.axis_size("xh") * lax.axis_size("xl")
    rows, blk = memory.shape[1:]
    t_rows, width = queries.shape[2:]
    depth = key_weight.shape[1]
    swap = [(0, 1), (1, 0)]
    n_y = lax.axis_size("y")
    length_tile = jnp.broadcast_to(target_lengths.astype(jnp.float32), (n_y, 8, 128))
    lengths = lax.all_to_all(length_tile, "y", 0, 0)
    loss_weight = float(n_y * t_rows) / jnp.sum(lengths[:, 0, 0])
    mine = memory[0].T
    along_z = lax.all_to_all(jnp.broadcast_to(mine, (n_z, blk, rows)), "z", 0, 0)
    along_z = along_z.reshape(n_z * blk, rows)
    own = lax.all_to_all(jnp.broadcast_to(along_z, (n_x, n_z * blk, rows)), X, 0, 0)
    other = lax.ppermute(own, "c", swap)
    half = (n_x, n_z, blk, rows)
    core = lax.axis_index("c").reshape(1)
    vmem = pl.BlockSpec(memory_space=pltpu.VMEM)
    smem = pl.BlockSpec(memory_space=pltpu.SMEM)
    context, keep, send = pl.pallas_call(
        local_kernel,
        out_shape=(
            jax.ShapeDtypeStruct((t_rows, width), jnp.bfloat16),
            jax.ShapeDtypeStruct(half, jnp.bfloat16),
            jax.ShapeDtypeStruct(half, jnp.bfloat16),
        ),
        in_specs=[smem, smem] + [vmem] * 6,
        out_specs=(vmem, vmem, vmem),
        scratch_shapes=[
            pltpu.VMEM((depth, rows), jnp.bfloat16),
            pltpu.VMEM((rows, depth), jnp.bfloat16),
            pltpu.VMEM((rows, width), jnp.bfloat16),
            pltpu.VMEM((rows, width), jnp.bfloat16),
        ],
        compiler_params=pltpu.CompilerParams(vmem_limit_bytes=24 << 20),
        cost_estimate=pl.CostEstimate(flops=2500000000, bytes_accessed=8 << 20, transcendentals=1 << 17),
    )(
        core, target_lengths, own.reshape(half), other.reshape(half),
        key_weight[0], value_weight[0], queries[0, 0], cotangent[0, 0],
    )
    got = lax.ppermute(send, "c", swap)
    pair = (keep.astype(jnp.float32) + got.astype(jnp.float32)).astype(jnp.bfloat16)
    parts = lax.all_to_all(pair.reshape(n_x, n_z * blk, rows), X, 0, 0)
    row_sum = jnp.sum(parts.astype(jnp.float32), axis=0).astype(jnp.bfloat16)
    parts = lax.all_to_all(row_sum.reshape(n_z, blk, rows), "z", 0, 0)
    own_grad = jnp.sum(parts.astype(jnp.float32), axis=0) * loss_weight
    return context[None, None], own_grad.T[None]


def solution(mesh):
    fine = Mesh(mesh.devices.reshape(16, 2, 4, 2, 2), ("z", "xh", "y", "xl", "c"))
    layers, heads, features = ("z", "xh"), ("xl", "c"), ("z", "xh", "xl", "c")
    return jax.shard_map(
        on_device,
        mesh=fine,
        in_specs=(
            P("y", None, features),
            P(layers, None, heads),
            P(layers, None, heads),
            P(layers, "y", None, heads),
            P(layers, "y", None, heads),
            P("y"),
        ),
        out_specs=(P(layers, "y", None, heads), P("y", None, features)),
        check_vma=False,
    )
```

time: 431 us -> 101 us (0.23)
  the two profiles are of different devices: /device:TPU:8 before, /device:TPU:32 now
where the time goes in v1:
time: 101 us
  blocking collectives  41.4 us (41%)
  waiting for transfers between devices  28.8 us (29%)
  starting transfers between devices  17.1 us (17%)
  local copies, waits for them, and re-layouts  4.99 us (5%)
  Pallas kernels  3.67 us (4%)
  other arithmetic  2.94 us (3%)
  between operations  2.03 us (2%)
    all_to_all x1, blocking collectives, on_device(): lax.all_to_all(jnp.broadcast_to(mine, (n_z, blk, rows)), 'z', 0, 0)  29.2 us
    all_to_all x1, blocking collectives, on_device(): lax.all_to_all(jnp.broadcast_to(along_z, (n_x, n_z * blk, rows)), X, 0, 0)  12.2 us
    all_to_all x1, waiting for transfers between devices, on_device(): parts = lax.all_to_all(row_sum.reshape(n_z, blk, rows), 'z', 0, 0)  11.2 us
    all_to_all x1, waiting for transfers between devices, on_device(): parts = lax.all_to_all(pair.reshape(n_x, n_z * blk, rows), X, 0, 0)  10 us
    all_to_all x1, starting transfers between devices, on_device(): parts = lax.all_to_all(row_sum.reshape(n_z, blk, rows), 'z', 0, 0)  5.18 us
    all_to_all x1, waiting for transfers between devices, on_device(): lengths = lax.all_to_all(length_tile, 'y', 0, 0)  4.62 us
    all_to_all x1, starting transfers between devices, on_device(): lengths = lax.all_to_all(length_tile, 'y', 0, 0)  4.46 us
    pallas_call x1, Pallas kernels, on_device(): pl.pallas_call(local_kernel, out_shape=(jax.ShapeDtypeStruct((t_rows, wid...  3.67 us
  transfers between devices with their start and end apart: 5, of which 5 were waited for; matrix products, arithmetic and copies ran while one was open for 1% of the time, Pallas kernels for 0%

profile of v1, /device:TPU:32, one launch (start us, length us, event | category | flops | bytes accessed | tf_op | source)
XLA Modules:
  0.0 100.9 jit_solution(1725908737838008895)
XLA Ops:
  0.6 0.0 copy-start
  0.6 0.9 broadcast_in_dim.17
  1.5 29.2 %all_to_all.25 = bf16[16,16,256]{2,1,0:T(8,128)(2,1)S(1)} all-to-all(bf16[16,16,256]{2,1,0:T(8,128)(2,1)S(1)} %broadcast_in_dim.17), channel_id=1, replica_groups=mesh['z'=16,'xh'=2,'y'=4,'xl'=2,'c'=2] {'z'}, dimensions={0} | all-to-all | bytes 262144 | tf_op jit(solution)/shard_map/all_to_all | solution.py:77
  30.8 12.2 %all_to_all.26 = bf16[4,256,256]{2,1,0:T(8,128)(2,1)S(1)} all-to-all(bf16[4,256,256]{2,1,0:T(8,128)(2,1)S(1)} %broadcast_in_dim.18), channel_id=1, replica_groups=mesh['z'=16,'xh'=2,'y'=4,'xl'=2,'c'=2] {'xh','xl'}, dimensions={0} | all-to-all | bytes 1048576 | tf_op jit(solution)/shard_map/all_to_all | solution.py:79
  42.9 1.9 %collective-permute-start = (bf16[4,256,256]{2,1,0:T(8,128)(2,1)S(1)}, bf16[4,256,256]{2,1,0:T(8,128)(2,1)S(1)}, u32[]{:S(2)}, u32[]{:S(2)}) collective-permute-start(bf16[4,256,256]{2,1,0:T(8,128)(2,1)S(1)} %all_to_all.26), channel_id=1, source_target_pairs={{0,1},{1,0},{2,3},{3,2},{4,5},{5,4},{6,7},{7,6},{8,9},{9,8},{10,11... | collective-permute-start | bytes 1572872 | tf_op jit(solution)/shard_map/ppermute | solution.py:80
  45.5 1.2 %collective-permute-done = bf16[4,256,256]{2,1,0:T(8,128)(2,1)S(1)} collective-permute-done((bf16[4,256,256]{2,1,0:T(8,128)(2,1)S(1)}, bf16[4,256,256]{2,1,0:T(8,128)(2,1)S(1)}, u32[]{:S(2)}, u32[]{:S(2)}) %collective-permute-start) | collective-permute-done | bytes 524320 | tf_op jit(solution)/shard_map/ppermute | solution.py:80
  46.7 0.0 copy-done
  46.7 0.0 copy-start.1
  46.7 1.6 %copy-done.1 = bf16[1,2048,512]{2,1,0:T(8,128)(2,1)S(1)} copy-done((bf16[1,2048,512]{2,1,0:T(8,128)(2,1)S(1)}, bf16[1,2048,512]{2,1,0:T(8,128)(2,1)}, u32[]{:S(2)}) %copy-start.1) | copy-done | bytes 2097176
  48.3 0.0 copy-start.2
  48.3 0.9 copy-done.2
  49.3 0.0 copy-start.3
  49.3 0.9 copy-done.3
  50.2 3.7 %shard_map.77 = (bf16[256,512]{1,0:T(8,128)(2,1)}, bf16[4,16,16,256]{3,2,1,0:T(8,128)(2,1)S(1)}, bf16[4,16,16,256]{3,2,1,0:T(8,128)(2,1)S(1)}) custom-call(s32[1]{0:T(128)} %bitcast.core_ref, s32[1]{0:T(128)S(6)} %copy.10.length_ref, bf16[4,16,16,256]{3,2,1,0:T(8,128)(2,1)S(1)} %bitcast.19, bf16[4,16,16,256]{3,2,1,0:T(8,128)(2,1)S(1)} %bitcast.22, ...), custom_call_target="tpu_custom_call" | custom-call | flops 2500000000 | bytes 8388608 | tf_op jit(solution)/shard_map/pallas_call | solution.py:85
  53.9 2.1 %collective-permute-start.1 = (bf16[4,16,16,256]{3,2,1,0:T(8,128)(2,1)S(1)}, bf16[4,16,16,256]{3,2,1,0:T(8,128)(2,1)S(1)}, u32[]{:S(2)}, u32[]{:S(2)}) collective-permute-start(bf16[4,16,16,256]{3,2,1,0:T(8,128)(2,1)S(1)} %get-tuple-element.7), channel_id=1, source_target_pairs={{0,1},{1,0},{2,3},{3,2},{4,5},{5,4},{6,7},{7,6},{8,9},{9,8},{10,11... | collective-permute-start | bytes 1572872 | tf_op jit(solution)/shard_map/ppermute | solution.py:106
  56.0 1.7 %collective-permute-done.1 = bf16[4,16,16,256]{3,2,1,0:T(8,128)(2,1)S(1)} collective-permute-done((bf16[4,16,16,256]{3,2,1,0:T(8,128)(2,1)S(1)}, bf16[4,16,16,256]{3,2,1,0:T(8,128)(2,1)S(1)}, u32[]{:S(2)}, u32[]{:S(2)}) %collective-permute-start.1) | collective-permute-done | bytes 524320 | tf_op jit(solution)/shard_map/ppermute | solution.py:106
  57.7 1.0 add_convert_fusion
  58.7 3.5 %all-to-all-start.2 = ((bf16[4,256,256]{2,1,0:T(8,128)(2,1)}), bf16[4,256,256]{2,1,0:T(8,128)(2,1)S(1)}, u32[]{:S(2)}, u32[]{:S(2)}) async-start(bf16[4,256,256]{2,1,0:T(8,128)(2,1)} %bitcast.11), calls=%async_computation.2 | async-start | bytes 1048576 | tf_op jit(solution)/shard_map/all_to_all | solution.py:108
  62.1 10.0 %all-to-all-done.2 = bf16[4,256,256]{2,1,0:T(8,128)(2,1)S(1)} async-done(((bf16[4,256,256]{2,1,0:T(8,128)(2,1)}), bf16[4,256,256]{2,1,0:T(8,128)(2,1)S(1)}, u32[]{:S(2)}, u32[]{:S(2)}) %all-to-all-start.2) | async-done | bytes 524320 | tf_op jit(solution)/shard_map/all_to_all | solution.py:108
  72.2 0.6 broadcast_in_dim.20
  72.8 4.5 %all-to-all-start.4 = ((f32[4,8,128]{2,1,0:T(8,128)}), f32[4,8,128]{2,1,0:T(8,128)S(1)}, u32[]{:S(2)}, u32[]{:S(2)}) async-start(f32[4,8,128]{2,1,0:T(8,128)} %broadcast_in_dim.20), calls=%async_computation.4 | async-start | bytes 32768 | tf_op jit(solution)/shard_map/all_to_all | solution.py:74
  77.2 0.7 reduce_sum.30
  78.0 4.6 %all-to-all-done.4 = f32[4,8,128]{2,1,0:T(8,128)S(1)} async-done(((f32[4,8,128]{2,1,0:T(8,128)}), f32[4,8,128]{2,1,0:T(8,128)S(1)}, u32[]{:S(2)}, u32[]{:S(2)}) %all-to-all-start.4) | async-done | bytes 16416 | tf_op jit(solution)/shard_map/all_to_all | solution.py:74
  82.6 5.2 %all-to-all-start.3 = ((bf16[16,16,256]{2,1,0:T(8,128)(2,1)}), bf16[16,16,256]{2,1,0:T(8,128)(2,1)S(1)}, u32[]{:S(2)}, u32[]{:S(2)}) async-start(bf16[16,16,256]{2,1,0:T(8,128)(2,1)} %bitcast.12), calls=%async_computation.3 | async-start | bytes 262144 | tf_op jit(solution)/shard_map/all_to_all | solution.py:110
  87.8 0.6 slice_reduce_fusion
  89.1 11.2 %all-to-all-done.3 = bf16[16,16,256]{2,1,0:T(8,128)(2,1)S(1)} async-done(((bf16[16,16,256]{2,1,0:T(8,128)(2,1)}), bf16[16,16,256]{2,1,0:T(8,128)(2,1)S(1)}, u32[]{:S(2)}, u32[]{:S(2)}) %all-to-all-start.3) | async-done | bytes 131104 | tf_op jit(solution)/shard_map/all_to_all | solution.py:110
  100.3 0.6 multiply_bitcast_fusion
  (2 shorter events, 0.1 us)
Async XLA Ops:
  0.6 46.1 %copy-start = (bf16[1,2048,512]{2,1,0:T(8,128)(2,1)S(1)}, bf16[1,2048,512]{2,1,0:T(8,128)(2,1)}, u32[]{:S(2)}) copy-start(bf16[1,2048,512]{2,1,0:T(8,128)(2,1)} %param.7) | copy-start | bytes 6291460
  42.9 3.8 %collective-permute-start = (bf16[4,256,256]{2,1,0:T(8,128)(2,1)S(1)}, bf16[4,256,256]{2,1,0:T(8,128)(2,1)S(1)}, u32[]{:S(2)}, u32[]{:S(2)}) collective-permute-start(bf16[4,256,256]{2,1,0:T(8,128)(2,1)S(1)} %all_to_all.26), channel_id=1, source_target_pairs={{0,1},{1,0},{2,3},{3,2},{4,5},{5,4},{6,7},{7,6},{8,9},{9,8},{10,11... | collective-permute-start | bytes 1572872 | tf_op jit(solution)/shard_map/ppermute | solution.py:80
  46.7 1.6 %copy-start.1 = (bf16[1,2048,512]{2,1,0:T(8,128)(2,1)S(1)}, bf16[1,2048,512]{2,1,0:T(8,128)(2,1)}, u32[]{:S(2)}) copy-start(bf16[1,2048,512]{2,1,0:T(8,128)(2,1)} %param.8) | copy-start | bytes 6291460
  48.3 0.9 copy-start.2
  49.3 0.9 copy-start.3
  53.9 3.8 %collective-permute-start.1 = (bf16[4,16,16,256]{3,2,1,0:T(8,128)(2,1)S(1)}, bf16[4,16,16,256]{3,2,1,0:T(8,128)(2,1)S(1)}, u32[]{:S(2)}, u32[]{:S(2)}) collective-permute-start(bf16[4,16,16,256]{3,2,1,0:T(8,128)(2,1)S(1)} %get-tuple-element.7), channel_id=1, source_target_pairs={{0,1},{1,0},{2,3},{3,2},{4,5},{5,4},{6,7},{7,6},{8,9},{9,8},{10,11... | collective-permute-start | bytes 1572872 | tf_op jit(solution)/shard_map/ppermute | solution.py:106
  58.7 13.5 %all-to-all-start.2 = ((bf16[4,256,256]{2,1,0:T(8,128)(2,1)}), bf16[4,256,256]{2,1,0:T(8,128)(2,1)S(1)}, u32[]{:S(2)}, u32[]{:S(2)}) async-start(bf16[4,256,256]{2,1,0:T(8,128)(2,1)} %bitcast.11), calls=%async_computation.2 | async-start | bytes 1048576 | tf_op jit(solution)/shard_map/all_to_all | solution.py:108
  72.8 9.8 %all-to-all-start.4 = ((f32[4,8,128]{2,1,0:T(8,128)}), f32[4,8,128]{2,1,0:T(8,128)S(1)}, u32[]{:S(2)}, u32[]{:S(2)}) async-start(f32[4,8,128]{2,1,0:T(8,128)} %broadcast_in_dim.20), calls=%async_computation.4 | async-start | bytes 32768 | tf_op jit(solution)/shard_map/all_to_all | solution.py:74
  82.6 17.7 %all-to-all-start.3 = ((bf16[16,16,256]{2,1,0:T(8,128)(2,1)}), bf16[16,16,256]{2,1,0:T(8,128)(2,1)S(1)}, u32[]{:S(2)}, u32[]{:S(2)}) async-start(bf16[16,16,256]{2,1,0:T(8,128)(2,1)} %bitcast.12), calls=%async_computation.3 | async-start | bytes 262144 | tf_op jit(solution)/shard_map/all_to_all | solution.py:110

commit v2 on v1

--- a/solution.py
+++ b/solution.py
@@ -4,6 +4,7 @@
 from jax.experimental import pallas as pl
 from jax.experimental.pallas import tpu as pltpu
 from jax.sharding import Mesh, PartitionSpec as P
+
 
 HEAD_DIM = 256
 NT = (((1,), (1,)), ((), ()))
@@ -16,12 +17,19 @@
 
 
 def local_kernel(
-    core_ref, length_ref, own_ref, other_ref, wk_ref, wv_ref, q_ref, cot_ref,
-    context_ref, keep_ref, send_ref, mt_ref, m_ref, kg_ref, vg_ref,
+    core_ref, length_ref, own_ref, other_ref, wk_ref, wv_hbm, q_hbm, cot_hbm,
+    context_ref, keep_ref, send_ref,
+    mt_ref, m_ref, kg_ref, vg_ref, wv_ref, q_ref, cot_ref, sems,
 ):
+    loads = [
+        pltpu.make_async_copy(src, dst, sems.at[i])
+        for i, (src, dst) in enumerate(((q_hbm, q_ref), (wv_hbm, wv_ref), (cot_hbm, cot_ref)))
+    ]
+    for load in loads:
+        load.start()
     core = core_ref[0]
     length = length_ref[0]
-    n_x, n_z, blk, rows = own_ref.shape
+    n_x, n_z, blk, _ = own_ref.shape
     span = n_x * blk * 2
     width = wk_ref.shape[1]
     scale = HEAD_DIM ** (-0.5)
@@ -33,15 +41,20 @@
     for z in range(n_z):
         m_ref[:, z * span:(z + 1) * span] = mt_ref[z * span:(z + 1) * span, :].T
     keys = dot(m_ref[...], wk_ref[...]).astype(jnp.bfloat16)
-    values = dot(m_ref[...], wv_ref[...]).astype(jnp.bfloat16)
     t_rows = q_ref.shape[0]
     valid = lax.broadcasted_iota(jnp.int32, (t_rows, HEAD_DIM), 0) < length
-    for h in range(width // HEAD_DIM):
-        cols = slice(h * HEAD_DIM, (h + 1) * HEAD_DIM)
-        key, value, query = keys[:, cols], values[:, cols], q_ref[:, cols]
-        scores = dot(key, query, NT) * scale
+    heads = [slice(h, h + HEAD_DIM) for h in range(0, width, HEAD_DIM)]
+    loads[0].wait()
+    all_probs = []
+    for cols in heads:
+        scores = dot(keys[:, cols], q_ref[:, cols], NT) * scale
         weights = jnp.exp(scores - jnp.max(scores, axis=0, keepdims=True))
-        probs = weights / jnp.sum(weights, axis=0, keepdims=True)
+        all_probs.append(weights / jnp.sum(weights, axis=0, keepdims=True))
+    loads[1].wait()
+    values = dot(m_ref[...], wv_ref[...]).astype(jnp.bfloat16)
+    loads[2].wait()
+    for cols, probs in zip(heads, all_probs):
+        value = values[:, cols]
         probs_low = probs.astype(jnp.bfloat16)
         context = dot(probs_low, value, TN)
         context_ref[:, cols] = jnp.where(valid, context, 0.0).astype(jnp.bfloat16)
@@ -50,7 +63,7 @@
         prob_grad = dot(value, cot, NT)
         row_dot = jnp.sum(probs * prob_grad, axis=0, keepdims=True)
         score_grad = (probs * (prob_grad - row_dot) * scale).astype(jnp.bfloat16)
-        kg_ref[:, cols] = dot(score_grad, query).astype(jnp.bfloat16)
+        kg_ref[:, cols] = dot(score_grad, q_ref[:, cols]).astype(jnp.bfloat16)
     first = core == 0
     for z in range(0, n_z, 2):
         at = slice(z * span, (z + 2) * span)
@@ -70,11 +83,12 @@
     depth = key_weight.shape[1]
     swap = [(0, 1), (1, 0)]
     n_y = lax.axis_size("y")
-    length_tile = jnp.broadcast_to(target_lengths.astype(jnp.float32), (n_y, 8, 128))
-    lengths = lax.all_to_all(length_tile, "y", 0, 0)
-    loss_weight = float(n_y * t_rows) / jnp.sum(lengths[:, 0, 0])
+    tokens = jnp.broadcast_to(target_lengths.astype(jnp.float32), (8, 128))
+    tokens = tokens + lax.ppermute(tokens, "y", [(y, y ^ 1) for y in range(n_y)])
     mine = memory[0].T
-    along_z = lax.all_to_all(jnp.broadcast_to(mine, (n_z, blk, rows)), "z", 0, 0)
+    to_z = jnp.broadcast_to(mine, (n_z, blk, rows))
+    along_z = lax.all_to_all(to_z, "z", 0, 0)
+    along_z, tokens = lax.optimization_barrier((along_z, tokens))
     along_z = along_z.reshape(n_z * blk, rows)
     own = lax.all_to_all(jnp.broadcast_to(along_z, (n_x, n_z * blk, rows)), X, 0, 0)
     other = lax.ppermute(own, "c", swap)
@@ -89,25 +103,31 @@
             jax.ShapeDtypeStruct(half, jnp.bfloat16),
             jax.ShapeDtypeStruct(half, jnp.bfloat16),
         ),
-        in_specs=[smem, smem] + [vmem] * 6,
+        in_specs=[smem, smem] + [vmem] * 3 + [pl.BlockSpec(memory_space=pltpu.HBM)] * 3,
         out_specs=(vmem, vmem, vmem),
         scratch_shapes=[
             pltpu.VMEM((depth, rows), jnp.bfloat16),
             pltpu.VMEM((rows, depth), jnp.bfloat16),
             pltpu.VMEM((rows, width), jnp.bfloat16),
             pltpu.VMEM((rows, width), jnp.bfloat16),
+            pltpu.VMEM((depth, width), jnp.bfloat16),
+            pltpu.VMEM((t_rows, width), jnp.bfloat16),
+            pltpu.VMEM((t_rows, width), jnp.bfloat16),
+            pltpu.SemaphoreType.DMA((3,)),
         ],
         compiler_params=pltpu.CompilerParams(vmem_limit_bytes=24 << 20),
         cost_estimate=pl.CostEstimate(flops=2500000000, bytes_accessed=8 << 20, transcendentals=1 << 17),
     )(
         core, target_lengths, own.reshape(half), other.reshape(half),
-        key_weight[0], value_weight[0], queries[0, 0], cotangent[0, 0],
+        key_weight[0], *[pltpu.with_memory_space_constraint(a, pltpu.HBM) for a in (value_weight[0], queries[0, 0], cotangent[0, 0])],
     )
     got = lax.ppermute(send, "c", swap)
     pair = (keep.astype(jnp.float32) + got.astype(jnp.float32)).astype(jnp.bfloat16)
     parts = lax.all_to_all(pair.reshape(n_x, n_z * blk, rows), X, 0, 0)
     row_sum = jnp.sum(parts.astype(jnp.float32), axis=0).astype(jnp.bfloat16)
     parts = lax.all_to_all(row_sum.reshape(n_z, blk, rows), "z", 0, 0)
+    tokens = tokens + lax.ppermute(tokens, "y", [(y, y ^ 2) for y in range(n_y)])
+    loss_weight = float(n_y * t_rows) / tokens[0, 0]
     own_grad = jnp.sum(parts.astype(jnp.float32), axis=0) * loss_weight
     return context[None, None], own_grad.T[None]
 

time: 101 us -> 89.8 us (0.89)
  the two profiles are of different devices: /device:TPU:32 before, /device:TPU:8 now
where the time goes in v2:
time: 89.8 us; the launch traced here: 89.2 us
  starting transfers between devices  30.3 us (34%)
  blocking collectives  24.6 us (27%)
  waiting for transfers between devices  24.2 us (27%)
  Pallas kernels  4.42 us (5%)
  local copies, waits for them, and re-layouts  2.07 us (2%)
  between operations  2.06 us (2%)
  other arithmetic  1.54 us (2%)
    all_to_all x1, starting transfers between devices, on_device(): along_z = lax.all_to_all(to_z, 'z', 0, 0)  15.2 us
    all_to_all x1, blocking collectives, on_device(): parts = lax.all_to_all(pair.reshape(n_x, n_z * blk, rows), X, 0, 0)  12.5 us
    all_to_all x1, blocking collectives, on_device(): lax.all_to_all(jnp.broadcast_to(along_z, (n_x, n_z * blk, rows)), X, 0, 0)  12.2 us
    all_to_all x1, waiting for transfers between devices, on_device(): along_z = lax.all_to_all(to_z, 'z', 0, 0)  8.62 us
    all_to_all x1, waiting for transfers between devices, on_device(): parts = lax.all_to_all(row_sum.reshape(n_z, blk, rows), 'z', 0, 0)  6.02 us
    all_to_all x1, starting transfers between devices, on_device(): parts = lax.all_to_all(row_sum.reshape(n_z, blk, rows), 'z', 0, 0)  4.59 us
    pallas_call x1, Pallas kernels, on_device(): pl.pallas_call(local_kernel, out_shape=(jax.ShapeDtypeStruct((t_rows, wid...  4.42 us
    ppermute x1, starting transfers between devices, on_device(): lax.ppermute(tokens, 'y', [(y, y ^ 2) for y in range(n_y)])  4.2 us
  transfers between devices with their start and end apart: 6, of which 6 were waited for; matrix products, arithmetic and copies ran while one was open for 1% of the time, Pallas kernels for 0%

profile of v2, /device:TPU:8, one launch (start us, length us, event | category | flops | bytes accessed | tf_op | source)
XLA Modules:
  0.0 89.2 jit_solution(15974476075064123927)
XLA Ops:
  0.6 0.0 copy-start
  0.6 1.5 %broadcast_in_dim.17 = bf16[16,16,256]{2,1,0:T(8,128)(2,1)} broadcast(bf16[16,256]{1,0:T(8,128)(2,1)} %bitcast.25), dimensions={1,2} | broadcast | bytes 139264 | tf_op jit(solution)/shard_map/broadcast_in_dim | solution.py:89
  2.1 15.2 %all-to-all-start = ((bf16[16,16,256]{2,1,0:T(8,128)(2,1)}), bf16[16,16,256]{2,1,0:T(8,128)(2,1)S(1)}, u32[]{:S(2)}, u32[]{:S(2)}) async-start(bf16[16,16,256]{2,1,0:T(8,128)(2,1)} %broadcast_in_dim.17), calls=%async_computation | async-start | bytes 262144 | tf_op jit(solution)/shard_map/all_to_all | solution.py:90
  18.0 2.4 %collective-permute-start = (f32[8,128]{1,0:T(8,128)S(1)}, f32[8,128]{1,0:T(8,128)S(1)}, u32[]{:S(2)}, u32[]{:S(2)}) collective-permute-start(f32[8,128]{1,0:T(8,128)S(1)} %broadcast_in_dim.18), channel_id=1, source_target_pairs={{0,4},{4,0},{8,12},{12,8},{1,5},{5,1},{9,13},{13,9},{2,6},{6,2},{1... | collective-permute-start | bytes 12296 | tf_op jit(solution)/shard_map/ppermute | solution.py:87
  20.4 3.1 %collective-permute-done = f32[8,128]{1,0:T(8,128)S(1)} collective-permute-done((f32[8,128]{1,0:T(8,128)S(1)}, f32[8,128]{1,0:T(8,128)S(1)}, u32[]{:S(2)}, u32[]{:S(2)}) %collective-permute-start) | collective-permute-done | bytes 4128 | tf_op jit(solution)/shard_map/ppermute | solution.py:87
  23.5 8.6 %all-to-all-done = bf16[16,16,256]{2,1,0:T(8,128)(2,1)S(1)} async-done(((bf16[16,16,256]{2,1,0:T(8,128)(2,1)}), bf16[16,16,256]{2,1,0:T(8,128)(2,1)S(1)}, u32[]{:S(2)}, u32[]{:S(2)}) %all-to-all-start) | async-done | bytes 131104 | tf_op jit(solution)/shard_map/all_to_all | solution.py:90
  32.2 12.2 %all_to_all.20 = bf16[4,256,256]{2,1,0:T(8,128)(2,1)S(1)} all-to-all(bf16[4,256,256]{2,1,0:T(8,128)(2,1)S(1)} %broadcast_in_dim.19), channel_id=1, replica_groups=mesh['z'=16,'xh'=2,'y'=4,'xl'=2,'c'=2] {'xh','xl'}, dimensions={0} | all-to-all | bytes 1048576 | tf_op jit(solution)/shard_map/all_to_all | solution.py:93
  44.4 1.9 %collective-permute-start.1 = (bf16[4,256,256]{2,1,0:T(8,128)(2,1)S(1)}, bf16[4,256,256]{2,1,0:T(8,128)(2,1)S(1)}, u32[]{:S(2)}, u32[]{:S(2)}) collective-permute-start(bf16[4,256,256]{2,1,0:T(8,128)(2,1)S(1)} %all_to_all.20), channel_id=1, source_target_pairs={{0,1},{1,0},{2,3},{3,2},{4,5},{5,4},{6,7},{7,6},{8,9},{9,8},{10,11... | collective-permute-start | bytes 1572872 | tf_op jit(solution)/shard_map/ppermute | solution.py:94
  46.3 1.9 %collective-permute-done.1 = bf16[4,256,256]{2,1,0:T(8,128)(2,1)S(1)} collective-permute-done((bf16[4,256,256]{2,1,0:T(8,128)(2,1)S(1)}, bf16[4,256,256]{2,1,0:T(8,128)(2,1)S(1)}, u32[]{:S(2)}, u32[]{:S(2)}) %collective-permute-start.1) | collective-permute-done | bytes 524320 | tf_op jit(solution)/shard_map/ppermute | solution.py:94
  48.1 0.0 copy-done
  48.1 4.4 %shard_map.77 = (bf16[256,512]{1,0:T(8,128)(2,1)}, bf16[4,16,16,256]{3,2,1,0:T(8,128)(2,1)S(1)}, bf16[4,16,16,256]{3,2,1,0:T(8,128)(2,1)S(1)}) custom-call(s32[1]{0:T(128)} %bitcast.core_ref, s32[1]{0:T(128)S(6)} %copy.8.length_ref, bf16[4,16,16,256]{3,2,1,0:T(8,128)(2,1)S(1)} %bitcast.20, bf16[4,16,16,256]{3,2,1,0:T(8,128)(2,1)S(1)} %bitcast.22, ...), custom_call_target="tpu_custom_call" | custom-call | flops 2500000000 | bytes 8388608 | tf_op jit(solution)/shard_map/pallas_call | solution.py:99
  52.6 2.0 %collective-permute-start.2 = (bf16[4,16,16,256]{3,2,1,0:T(8,128)(2,1)S(1)}, bf16[4,16,16,256]{3,2,1,0:T(8,128)(2,1)S(1)}, u32[]{:S(2)}, u32[]{:S(2)}) collective-permute-start(bf16[4,16,16,256]{3,2,1,0:T(8,128)(2,1)S(1)} %get-tuple-element.10), channel_id=1, source_target_pairs={{0,1},{1,0},{2,3},{3,2},{4,5},{5,4},{6,7},{7,6},{8,9},{9,8},{10,11... | collective-permute-start | bytes 1572872 | tf_op jit(solution)/shard_map/ppermute | solution.py:124
  54.6 1.8 %collective-permute-done.2 = bf16[4,16,16,256]{3,2,1,0:T(8,128)(2,1)S(1)} collective-permute-done((bf16[4,16,16,256]{3,2,1,0:T(8,128)(2,1)S(1)}, bf16[4,16,16,256]{3,2,1,0:T(8,128)(2,1)S(1)}, u32[]{:S(2)}, u32[]{:S(2)}) %collective-permute-start.2) | collective-permute-done | bytes 524320 | tf_op jit(solution)/shard_map/ppermute | solution.py:124
  56.4 0.2 add_convert_fusion
  56.5 12.5 %all_to_all.21 = bf16[4,256,256]{2,1,0:T(8,128)(2,1)S(1)} all-to-all(bf16[4,256,256]{2,1,0:T(8,128)(2,1)S(1)} %bitcast.23), channel_id=1, replica_groups=mesh['z'=16,'xh'=2,'y'=4,'xl'=2,'c'=2] {'xh','xl'}, dimensions={0} | all-to-all | bytes 1048576 | tf_op jit(solution)/shard_map/all_to_all | solution.py:126
  69.0 0.7 reduce_sum.21
  69.7 4.6 %all-to-all-start.3 = ((bf16[16,16,256]{2,1,0:T(8,128)(2,1)}), bf16[16,16,256]{2,1,0:T(8,128)(2,1)S(1)}, u32[]{:S(2)}, u32[]{:S(2)}) async-start(bf16[16,16,256]{2,1,0:T(8,128)(2,1)} %bitcast.13), calls=%async_computation.3 | async-start | bytes 262144 | tf_op jit(solution)/shard_map/all_to_all | solution.py:128
  74.3 4.2 %collective-permute-start.3 = (f32[8,128]{1,0:T(8,128)S(1)}, f32[8,128]{1,0:T(8,128)S(1)}, u32[]{:S(2)}, u32[]{:S(2)}) collective-permute-start(f32[8,128]{1,0:T(8,128)S(1)} %broadcast_add_fusion), channel_id=1, source_target_pairs={{0,8},{4,12},{8,0},{12,4},{1,9},{5,13},{9,1},{13,5},{2,10},{6,14},... | collective-permute-start | bytes 12296 | tf_op jit(solution)/shard_map/ppermute | solution.py:129
  78.6 2.8 %collective-permute-done.3 = f32[8,128]{1,0:T(8,128)S(1)} collective-permute-done((f32[8,128]{1,0:T(8,128)S(1)}, f32[8,128]{1,0:T(8,128)S(1)}, u32[]{:S(2)}, u32[]{:S(2)}) %collective-permute-start.3) | collective-permute-done | bytes 4128 | tf_op jit(solution)/shard_map/ppermute | solution.py:129
  81.4 0.5 slice.3
  82.6 6.0 %all-to-all-done.3 = bf16[16,16,256]{2,1,0:T(8,128)(2,1)S(1)} async-done(((bf16[16,16,256]{2,1,0:T(8,128)(2,1)}), bf16[16,16,256]{2,1,0:T(8,128)(2,1)S(1)}, u32[]{:S(2)}, u32[]{:S(2)}) %all-to-all-start.3) | async-done | bytes 131104 | tf_op jit(solution)/shard_map/all_to_all | solution.py:128
  88.6 0.6 multiply_bitcast_fusion
  (5 shorter events, 0.1 us)
Async XLA Ops:
  0.6 47.5 %copy-start = (bf16[1,2048,512]{2,1,0:T(8,128)(2,1)S(1)}, bf16[1,2048,512]{2,1,0:T(8,128)(2,1)}, u32[]{:S(2)}) copy-start(bf16[1,2048,512]{2,1,0:T(8,128)(2,1)} %param.7) | copy-start | bytes 6291460
  2.1 30.0 %all-to-all-start = ((bf16[16,16,256]{2,1,0:T(8,128)(2,1)}), bf16[16,16,256]{2,1,0:T(8,128)(2,1)S(1)}, u32[]{:S(2)}, u32[]{:S(2)}) async-start(bf16[16,16,256]{2,1,0:T(8,128)(2,1)} %broadcast_in_dim.17), calls=%async_computation | async-start | bytes 262144 | tf_op jit(solution)/shard_map/all_to_all | solution.py:90
  18.0 5.5 %collective-permute-start = (f32[8,128]{1,0:T(8,128)S(1)}, f32[8,128]{1,0:T(8,128)S(1)}, u32[]{:S(2)}, u32[]{:S(2)}) collective-permute-start(f32[8,128]{1,0:T(8,128)S(1)} %broadcast_in_dim.18), channel_id=1, source_target_pairs={{0,4},{4,0},{8,12},{12,8},{1,5},{5,1},{9,13},{13,9},{2,6},{6,2},{1... | collective-permute-start | bytes 12296 | tf_op jit(solution)/shard_map/ppermute | solution.py:87
  44.4 3.8 %collective-permute-start.1 = (bf16[4,256,256]{2,1,0:T(8,128)(2,1)S(1)}, bf16[4,256,256]{2,1,0:T(8,128)(2,1)S(1)}, u32[]{:S(2)}, u32[]{:S(2)}) collective-permute-start(bf16[4,256,256]{2,1,0:T(8,128)(2,1)S(1)} %all_to_all.20), channel_id=1, source_target_pairs={{0,1},{1,0},{2,3},{3,2},{4,5},{5,4},{6,7},{7,6},{8,9},{9,8},{10,11... | collective-permute-start | bytes 1572872 | tf_op jit(solution)/shard_map/ppermute | solution.py:94
  52.6 3.8 %collective-permute-start.2 = (bf16[4,16,16,256]{3,2,1,0:T(8,128)(2,1)S(1)}, bf16[4,16,16,256]{3,2,1,0:T(8,128)(2,1)S(1)}, u32[]{:S(2)}, u32[]{:S(2)}) collective-permute-start(bf16[4,16,16,256]{3,2,1,0:T(8,128)(2,1)S(1)} %get-tuple-element.10), channel_id=1, source_target_pairs={{0,1},{1,0},{2,3},{3,2},{4,5},{5,4},{6,7},{7,6},{8,9},{9,8},{10,11... | collective-permute-start | bytes 1572872 | tf_op jit(solution)/shard_map/ppermute | solution.py:124
  69.7 18.8 %all-to-all-start.3 = ((bf16[16,16,256]{2,1,0:T(8,128)(2,1)}), bf16[16,16,256]{2,1,0:T(8,128)(2,1)S(1)}, u32[]{:S(2)}, u32[]{:S(2)}) async-start(bf16[16,16,256]{2,1,0:T(8,128)(2,1)} %bitcast.13), calls=%async_computation.3 | async-start | bytes 262144 | tf_op jit(solution)/shard_map/all_to_all | solution.py:128
  74.3 7.0 %collective-permute-start.3 = (f32[8,128]{1,0:T(8,128)S(1)}, f32[8,128]{1,0:T(8,128)S(1)}, u32[]{:S(2)}, u32[]{:S(2)}) collective-permute-start(f32[8,128]{1,0:T(8,128)S(1)} %broadcast_add_fusion), channel_id=1, source_target_pairs={{0,8},{4,12},{8,0},{12,4},{1,9},{5,13},{9,1},{13,5},{2,10},{6,14},... | collective-permute-start | bytes 12296 | tf_op jit(solution)/shard_map/ppermute | solution.py:129

commit v3 on v1

v3 whole, which is shorter than its diff:
```python
import functools

import jax
import jax.numpy as jnp
from jax import lax
from jax.experimental import pallas as pl
from jax.experimental.pallas import tpu as pltpu
from jax.sharding import Mesh, PartitionSpec as P

HEAD_DIM = 256
NN = (((1,), (0,)), ((), ()))
NT = (((1,), (1,)), ((), ()))
TN = (((0,), (0,)), ((), ()))
X = ("xh", "xl")


def dot(a, b, dims=NN):
    return lax.dot_general(a, b, dims, preferred_element_type=jnp.float32)


def from_member(n, first):
    return [(first + i) % n for i in range(n)]


def feature_rows(ref, x, core, shape, order):
    n_x, _, blk, _ = shape
    return jnp.concatenate(
        [
            ref[pl.ds(pl.multiple_of((z * n_x + x) * 2 * blk + core * blk, blk), blk), :]
            for z in order
        ],
        axis=0,
    )


def own_kernel(
    order, core_ref, own_ref, wk_ref, wv_hbm, q_hbm, cot_hbm,
    wv_ref, q_ref, cot_ref, m_ref, key_part_ref, sems,
):
    loads = [
        pltpu.make_async_copy(src, dst, sems.at[i])
        for i, (src, dst) in enumerate(((wv_hbm, wv_ref), (q_hbm, q_ref), (cot_hbm, cot_ref)))
    ]
    for load in loads:
        load.start()
    n_x, n_z, blk, rows = own_ref.shape
    core = core_ref[0]
    total = None
    for x in range(n_x):
        mem = own_ref[x].reshape(n_z * blk, rows).T
        m_ref[:, x * n_z * blk:(x + 1) * n_z * blk] = mem
        part = dot(mem, feature_rows(wk_ref, x, core, own_ref.shape, order))
        total = part if total is None else total + part
    key_part_ref[...] = total
    for load in loads:
        load.wait()


def main_kernel(
    order, sum_order, core_ref, length_ref, other_ref, own_m_ref, key_part_ref, wk_ref, wv_ref, q_ref, cot_ref,
    context_hbm, send_ref, kg_ref, vg_ref, context_ref, sem,
):
    n_x, n_z, blk, rows = other_ref.shape
    core = core_ref[0]
    width = wk_ref.shape[1]
    scale = HEAD_DIM ** (-0.5)
    keys, values = key_part_ref[...], None
    for x in range(n_x):
        mem = other_ref[x].reshape(n_z * blk, rows).T
        keys = keys + dot(mem, feature_rows(wk_ref, x, 1 - core, other_ref.shape, order))
        part = dot(mem, feature_rows(wv_ref, x, 1 - core, other_ref.shape, order))
        values = part if values is None else values + part
        own = own_m_ref[:, x * n_z * blk:(x + 1) * n_z * blk]
        values = values + dot(own, feature_rows(wv_ref, x, core, other_ref.shape, order))
    keys, values = keys.astype(jnp.bfloat16), values.astype(jnp.bfloat16)
    t_rows = q_ref.shape[0]
    row = lax.broadcasted_iota(jnp.int32, (t_rows, HEAD_DIM), 0)
    valid = row.astype(jnp.float32) < length_ref[0:1, 0:1]
    heads = [slice(h, h + HEAD_DIM) for h in range(0, width, HEAD_DIM)]
    kept = []
    for cols in heads:
        scores = dot(keys[:, cols], q_ref[:, cols], NT) * scale
        weights = jnp.exp(scores - jnp.max(scores, axis=0, keepdims=True))
        probs = weights * (1.0 / jnp.sum(weights, axis=0, keepdims=True))
        probs_low = probs.astype(jnp.bfloat16)
        context = dot(probs_low, values[:, cols], TN)
        context_ref[:, cols] = jnp.where(valid, context, 0.0).astype(jnp.bfloat16)
        kept.append((probs, probs_low))
    out = pltpu.make_async_copy(context_ref, context_hbm, sem)
    out.start()
    for cols, (probs, probs_low) in zip(heads, kept):
        cot = jnp.where(valid, cot_ref[:, cols].astype(jnp.float32), 0.0).astype(jnp.bfloat16)
        vg_ref[:, cols] = dot(probs_low, cot).astype(jnp.bfloat16)
        prob_grad = dot(values[:, cols], cot, NT)
        row_dot = jnp.sum(probs * prob_grad, axis=0, keepdims=True)
        score_grad = (probs * (prob_grad - row_dot) * scale).astype(jnp.bfloat16)
        kg_ref[:, cols] = dot(score_grad, q_ref[:, cols]).astype(jnp.bfloat16)
    half_grad(sum_order, 1 - core, wk_ref, wv_ref, kg_ref, vg_ref, send_ref)
    out.wait()


def half_grad(order, core, wk_ref, wv_ref, kg_ref, vg_ref, out_ref):
    n_x, n_z, blk, rows = out_ref.shape
    kg, vg = kg_ref[...], vg_ref[...]
    for x in range(n_x):
        grad = dot(feature_rows(wk_ref, x, core, out_ref.shape, order), kg, NT)
        grad = grad + dot(feature_rows(wv_ref, x, core, out_ref.shape, order), vg, NT)
        out_ref[x] = grad.astype(jnp.bfloat16).reshape(n_z, blk, rows)


def keep_kernel(order, core_ref, wk_ref, wv_ref, kg_ref, vg_ref, keep_ref):
    half_grad(order, core_ref[0], wk_ref, wv_ref, kg_ref, vg_ref, keep_ref)


def on_device(memory, key_weight, value_weight, queries, cotangent, target_lengths):
    n_z, n_x = lax.axis_size("z"), lax.axis_size("xh") * lax.axis_size("xl")
    rows, blk = memory.shape[1:]
    t_rows, width = queries.shape[2:]
    depth = key_weight.shape[1]
    n_y = lax.axis_size("y")
    swap = [(0, 1), (1, 0)]
    half = (n_x, n_z, blk, rows)
    core = lax.axis_index("c").reshape(1)
    w_key = key_weight[0]
    w_value, query, cot = (
        pltpu.with_memory_space_constraint(a, pltpu.HBM)
        for a in (value_weight[0], queries[0, 0], cotangent[0, 0])
    )
    vmem = pl.BlockSpec(memory_space=pltpu.VMEM)
    smem = pl.BlockSpec(memory_space=pltpu.SMEM)
    hbm = pl.BlockSpec(memory_space=pltpu.HBM)
    params = pltpu.CompilerParams(vmem_limit_bytes=16 << 20)

    def low(*shape):
        return jax.ShapeDtypeStruct(shape, jnp.bfloat16)

    order = sum_order = from_member(n_z, n_z // 2)
    to_z = jnp.broadcast_to(memory[0].T, (n_z, blk, rows))
    along_z = lax.all_to_all(to_z, "z", 0, 0, axis_index_groups=[order])
    length = jnp.broadcast_to(target_lengths.astype(jnp.float32), (blk, rows))
    tokens = length + lax.ppermute(length, "y", [(y, y ^ 1) for y in range(n_y)])
    along_z, tokens = lax.optimization_barrier((along_z, tokens))
    along_z = along_z.reshape(n_z * blk, rows)
    to_x = jnp.broadcast_to(along_z, (n_x, n_z * blk, rows))
    own = lax.all_to_all(to_x, X, 0, 0)
    tokens = tokens + lax.ppermute(tokens, "y", [(y, y ^ 2) for y in range(n_y)])
    own, loss_weight = lax.optimization_barrier((own, float(n_y * t_rows) / tokens))
    other = lax.ppermute(own, "c", swap).reshape(half)
    w_value, query, cot, own_m, key_part = pl.pallas_call(
        functools.partial(own_kernel, order),
        out_shape=(
            low(depth, width), low(t_rows, width), low(t_rows, width), low(rows, depth // 2),
            jax.ShapeDtypeStruct((rows, width), jnp.float32),
        ),
        in_specs=[smem, vmem, vmem, hbm, hbm, hbm],
        out_specs=(vmem,) * 5,
        scratch_shapes=[pltpu.SemaphoreType.DMA((3,))],
        compiler_params=params,
        cost_estimate=pl.CostEstimate(flops=270000000, bytes_accessed=8 << 20, transcendentals=0),
    )(core, own.reshape(half), w_key, w_value, query, cot)
    context, send, key_grad, value_grad = pl.pallas_call(
        functools.partial(main_kernel, order, sum_order),
        out_shape=(low(t_rows, width), low(*half), low(rows, width), low(rows, width)),
        in_specs=[smem] + [vmem] * 8,
        out_specs=(hbm, vmem, vmem, vmem),
        scratch_shapes=[
            pltpu.VMEM((t_rows, width), jnp.bfloat16),
            pltpu.SemaphoreType.DMA,
        ],
        compiler_params=params,
        cost_estimate=pl.CostEstimate(flops=1700000000, bytes_accessed=8 << 20, transcendentals=1 << 17),
    )(core, length, other, own_m, key_part, w_key, w_value, query, cot)
    got = lax.ppermute(send, "c", swap)
    keep = pl.pallas_call(
        functools.partial(keep_kernel, sum_order),
        out_shape=low(*half),
        in_specs=[smem] + [vmem] * 4,
        out_specs=vmem,
        compiler_params=params,
        cost_estimate=pl.CostEstimate(flops=540000000, bytes_accessed=5 << 20, transcendentals=0),
    )(core, w_key, w_value, key_grad, value_grad)
    pair = (keep.astype(jnp.float32) + got.astype(jnp.float32)).astype(jnp.bfloat16)
    parts = lax.all_to_all(pair.reshape(n_x, n_z * blk, rows), X, 0, 0)
    row_sum = jnp.sum(parts.astype(jnp.float32), axis=0).astype(jnp.bfloat16)
    parts = lax.all_to_all(row_sum.reshape(n_z, blk, rows), "z", 0, 0, axis_index_groups=[sum_order])
    own_grad = jnp.sum(parts.astype(jnp.float32), axis=0) * loss_weight
    return context[None, None], own_grad.T[None]


def solution(mesh):
    fine = Mesh(mesh.devices.reshape(16, 2, 4, 2, 2), ("z", "xh", "y", "xl", "c"))
    layers, heads, features = ("z", "xh"), ("xl", "c"), ("z", "xh", "xl", "c")
    return jax.shard_map(
        on_device,
        mesh=fine,
        in_specs=(
            P("y", None, features),
            P(layers, None, heads),
            P(layers, None, heads),
            P(layers, "y", None, heads),
            P(layers, "y", None, heads),
            P("y"),
        ),
        out_specs=(P(layers, "y", None, heads), P("y", None, features)),
        check_vma=False,
    )
```

time: 101 us -> 84.3 us (0.83)
  the two profiles are of different devices: /device:TPU:32 before, /device:TPU:24 now
where the time goes in v3:
time: 84.3 us; the launch traced here: 83.8 us
  starting transfers between devices  33.2 us (39%)
  blocking collectives  30.6 us (36%)
  waiting for transfers between devices  9.74 us (12%)
  Pallas kernels  5.63 us (7%)
  local copies, waits for them, and re-layouts  2.34 us (3%)
  between operations  1.39 us (2%)
  other arithmetic  0.88 us (1%)
    all_to_all x1, starting transfers between devices, on_device(): along_z = lax.all_to_all(to_z, 'z', 0, 0, axis_index_groups=[order])  18.9 us
    all_to_all x1, blocking collectives, on_device(): lax.all_to_all(row_sum.reshape(n_z, blk, rows), 'z', 0, 0, axis_index_gro...  17.7 us
    all_to_all x1, blocking collectives, on_device(): parts = lax.all_to_all(pair.reshape(n_x, n_z * blk, rows), X, 0, 0)  12.8 us
    all_to_all x1, starting transfers between devices, on_device(): own = lax.all_to_all(to_x, X, 0, 0)  4.29 us
    ppermute x1, waiting for transfers between devices, on_device(): lax.ppermute(tokens, 'y', [(y, y ^ 2) for y in range(n_y)])  3.99 us
    ppermute x1, starting transfers between devices, on_device(): lax.ppermute(tokens, 'y', [(y, y ^ 2) for y in range(n_y)])  3.13 us
    ppermute x1, waiting for transfers between devices, on_device(): lax.ppermute(length, 'y', [(y, y ^ 1) for y in range(n_y)])  2.97 us
    pallas_call x1, Pallas kernels, on_device(): pl.pallas_call(functools.partial(main_kernel, order, sum_order), out_shap...  2.96 us
  transfers between devices with their start and end apart: 6, of which 5 were waited for; matrix products, arithmetic and copies ran while one was open for 0% of the time, Pallas kernels for 3%

profile of v3, /device:TPU:24, one launch (start us, length us, event | category | flops | bytes accessed | tf_op | source)
XLA Modules:
  0.0 83.8 jit_solution(14683502418412053955)
XLA Ops:
  0.6 0.0 copy-start
  0.6 1.5 %broadcast_in_dim.18 = bf16[16,16,256]{2,1,0:T(8,128)(2,1)} broadcast(bf16[16,256]{1,0:T(8,128)(2,1)} %bitcast.30), dimensions={1,2} | broadcast | bytes 139264 | tf_op jit(solution)/shard_map/broadcast_in_dim | solution.py:138
  2.1 18.9 %all-to-all-start = ((bf16[16,16,256]{2,1,0:T(8,128)(2,1)}), bf16[16,16,256]{2,1,0:T(8,128)(2,1)S(1)}, u32[]{:S(2)}, u32[]{:S(2)}) async-start(bf16[16,16,256]{2,1,0:T(8,128)(2,1)} %broadcast_in_dim.18), calls=%async_computation | async-start | bytes 262144 | tf_op jit(solution)/shard_map/all_to_all | solution.py:139
  21.7 2.7 %collective-permute-start = (f32[16,256]{1,0:T(8,128)S(1)}, f32[16,256]{1,0:T(8,128)S(1)}, u32[]{:S(2)}, u32[]{:S(2)}) collective-permute-start(f32[16,256]{1,0:T(8,128)S(1)} %broadcast_in_dim.17.length_ref), channel_id=1, source_target_pairs={{0,4},{4,0},{8,12},{12,8},{1,5},{5,1},{9,13},{13,9},{2,6},{6,2},{1... | collective-permute-start | bytes 49160 | tf_op jit(solution)/shard_map/ppermute | solution.py:141
  24.3 3.0 %collective-permute-done = f32[16,256]{1,0:T(8,128)S(1)} collective-permute-done((f32[16,256]{1,0:T(8,128)S(1)}, f32[16,256]{1,0:T(8,128)S(1)}, u32[]{:S(2)}, u32[]{:S(2)}) %collective-permute-start) | collective-permute-done | bytes 16416 | tf_op jit(solution)/shard_map/ppermute | solution.py:141
  27.3 0.2 all-to-all-done
  27.5 0.8 broadcast_in_dim.19
  28.3 4.3 %all-to-all-start.1 = ((bf16[4,256,256]{2,1,0:T(8,128)(2,1)}), bf16[4,256,256]{2,1,0:T(8,128)(2,1)S(1)}, u32[]{:S(2)}, u32[]{:S(2)}) async-start(bf16[4,256,256]{2,1,0:T(8,128)(2,1)} %broadcast_in_dim.19), calls=%async_computation.1 | async-start | bytes 1048576 | tf_op jit(solution)/shard_map/all_to_all | solution.py:145
  32.6 3.1 %collective-permute-start.1 = (f32[16,256]{1,0:T(8,128)S(1)}, f32[16,256]{1,0:T(8,128)S(1)}, u32[]{:S(2)}, u32[]{:S(2)}) collective-permute-start(f32[16,256]{1,0:T(8,128)S(1)} %broadcast_add_fusion), channel_id=1, source_target_pairs={{0,8},{4,12},{8,0},{12,4},{1,9},{5,13},{9,1},{13,5},{2,10},{6,14},... | collective-permute-start | bytes 49160 | tf_op jit(solution)/shard_map/ppermute | solution.py:146
  35.8 4.0 %collective-permute-done.1 = f32[16,256]{1,0:T(8,128)S(1)} collective-permute-done((f32[16,256]{1,0:T(8,128)S(1)}, f32[16,256]{1,0:T(8,128)S(1)}, u32[]{:S(2)}, u32[]{:S(2)}) %collective-permute-start.1) | collective-permute-done | bytes 16416 | tf_op jit(solution)/shard_map/ppermute | solution.py:146
  39.8 1.8 %all-to-all-done.1 = bf16[4,256,256]{2,1,0:T(8,128)(2,1)S(1)} async-done(((bf16[4,256,256]{2,1,0:T(8,128)(2,1)}), bf16[4,256,256]{2,1,0:T(8,128)(2,1)S(1)}, u32[]{:S(2)}, u32[]{:S(2)}) %all-to-all-start.1) | async-done | bytes 524320 | tf_op jit(solution)/shard_map/all_to_all | solution.py:145
  41.6 1.9 %collective-permute-start.2 = (bf16[4,256,256]{2,1,0:T(8,128)(2,1)S(1)}, bf16[4,256,256]{2,1,0:T(8,128)(2,1)S(1)}, u32[]{:S(2)}, u32[]{:S(2)}) collective-permute-start(bf16[4,256,256]{2,1,0:T(8,128)(2,1)S(1)} %all-to-all-done.1), channel_id=1, source_target_pairs={{0,1},{1,0},{2,3},{3,2},{4,5},{5,4},{6,7},{7,6},{8,9},{9,8},{10,11... | collective-permute-start | bytes 1572872 | tf_op jit(solution)/shard_map/ppermute | solution.py:148
  43.5 0.0 copy-done
  43.5 1.9 %shard_map.77 = (bf16[2048,512]{1,0:T(8,128)(2,1)S(1)}, bf16[256,512]{1,0:T(8,128)(2,1)S(1)}, bf16[256,512]{1,0:T(8,128)(2,1)S(1)}, bf16[256,1024]{1,0:T(8,128)(2,1)S(1)}, f32[256,512]{1,0:T(8,128)S(1)}) custom-call(s32[1]{0:T(128)} %bitcast.core_ref, bf16[4,16,16,256]{3,2,1,0:T(8,128)(2,1)S(1)} %bitcast.22, bf16[2048,512]{1,0:T(8,128)(2,1)S(1)} %bitcast.19, ...), custom_call_target="tpu_custom_call" | custom-call | flops 270000000 | bytes 8388608 | tf_op jit(solution)/shard_map/pallas_call | solution.py:149
  45.4 0.0 collective-permute-done.2
  45.4 3.0 %shard_map.78 = (bf16[256,512]{1,0:T(8,128)(2,1)}, bf16[4,16,16,256]{3,2,1,0:T(8,128)(2,1)S(1)}, bf16[256,512]{1,0:T(8,128)(2,1)S(1)}, bf16[256,512]{1,0:T(8,128)(2,1)S(1)}) custom-call(s32[1]{0:T(128)} %bitcast.core_ref, f32[16,256]{1,0:T(8,128)S(1)} %broadcast_in_dim.17.length_ref, bf16[4,16,16,256]{3,2,1,0:T(8,128)(2,1)S(1)} %bitcast.23, ...), custom_call_target="tpu_custom_call" | custom-call | flops 1700000000 | bytes 8388608 | tf_op jit(solution)/shard_map/pallas_call | solution.py:161
  48.4 2.4 %collective-permute-start.3 = (bf16[4,16,16,256]{3,2,1,0:T(8,128)(2,1)S(1)}, bf16[4,16,16,256]{3,2,1,0:T(8,128)(2,1)S(1)}, u32[]{:S(2)}, u32[]{:S(2)}) collective-permute-start(bf16[4,16,16,256]{3,2,1,0:T(8,128)(2,1)S(1)} %get-tuple-element.26), channel_id=1, source_target_pairs={{0,1},{1,0},{2,3},{3,2},{4,5},{5,4},{6,7},{7,6},{8,9},{9,8},{10,11... | collective-permute-start | bytes 1572872 | tf_op jit(solution)/shard_map/ppermute | solution.py:173
  50.8 0.7 shard_map.79
  51.6 0.8 collective-permute-done.3
  52.3 0.2 add_convert_fusion
  52.5 12.8 %all_to_all.20 = bf16[4,256,256]{2,1,0:T(8,128)(2,1)S(1)} all-to-all(bf16[4,256,256]{2,1,0:T(8,128)(2,1)S(1)} %bitcast.24), channel_id=1, replica_groups=mesh['z'=16,'xh'=2,'y'=4,'xl'=2,'c'=2] {'xh','xl'}, dimensions={0} | all-to-all | bytes 1048576 | tf_op jit(solution)/shard_map/all_to_all | solution.py:183
  65.3 0.1 reduce_sum.21
  65.4 17.7 %all_to_all.21 = bf16[16,16,256]{2,1,0:T(8,128)(2,1)S(1)} all-to-all(bf16[16,16,256]{2,1,0:T(8,128)(2,1)S(1)} %bitcast.27), channel_id=1, replica_groups={{256,288,320,352,384,416,448,480,0,32,64,96,128,160,192,224},{257,289,3..., dimensions={0} | all-to-all | bytes 262144 | tf_op jit(solution)/shard_map/all_to_all | solution.py:185
  83.2 0.6 multiply_bitcast_fusion
  (4 shorter events, 0.0 us)
Async XLA Ops:
  0.6 42.9 %copy-start = (bf16[1,2048,512]{2,1,0:T(8,128)(2,1)S(1)}, bf16[1,2048,512]{2,1,0:T(8,128)(2,1)}, u32[]{:S(2)}) copy-start(bf16[1,2048,512]{2,1,0:T(8,128)(2,1)} %param.7) | copy-start | bytes 6291460
  2.1 25.4 %all-to-all-start = ((bf16[16,16,256]{2,1,0:T(8,128)(2,1)}), bf16[16,16,256]{2,1,0:T(8,128)(2,1)S(1)}, u32[]{:S(2)}, u32[]{:S(2)}) async-start(bf16[16,16,256]{2,1,0:T(8,128)(2,1)} %broadcast_in_dim.18), calls=%async_computation | async-start | bytes 262144 | tf_op jit(solution)/shard_map/all_to_all | solution.py:139
  21.7 5.6 %collective-permute-start = (f32[16,256]{1,0:T(8,128)S(1)}, f32[16,256]{1,0:T(8,128)S(1)}, u32[]{:S(2)}, u32[]{:S(2)}) collective-permute-start(f32[16,256]{1,0:T(8,128)S(1)} %broadcast_in_dim.17.length_ref), channel_id=1, source_target_pairs={{0,4},{4,0},{8,12},{12,8},{1,5},{5,1},{9,13},{13,9},{2,6},{6,2},{1... | collective-permute-start | bytes 49160 | tf_op jit(solution)/shard_map/ppermute | solution.py:141
  28.3 13.2 %all-to-all-start.1 = ((bf16[4,256,256]{2,1,0:T(8,128)(2,1)}), bf16[4,256,256]{2,1,0:T(8,128)(2,1)S(1)}, u32[]{:S(2)}, u32[]{:S(2)}) async-start(bf16[4,256,256]{2,1,0:T(8,128)(2,1)} %broadcast_in_dim.19), calls=%async_computation.1 | async-start | bytes 1048576 | tf_op jit(solution)/shard_map/all_to_all | solution.py:145
  32.6 7.1 %collective-permute-start.1 = (f32[16,256]{1,0:T(8,128)S(1)}, f32[16,256]{1,0:T(8,128)S(1)}, u32[]{:S(2)}, u32[]{:S(2)}) collective-permute-start(f32[16,256]{1,0:T(8,128)S(1)} %broadcast_add_fusion), channel_id=1, source_target_pairs={{0,8},{4,12},{8,0},{12,4},{1,9},{5,13},{9,1},{13,5},{2,10},{6,14},... | collective-permute-start | bytes 49160 | tf_op jit(solution)/shard_map/ppermute | solution.py:146
  41.6 3.9 %collective-permute-start.2 = (bf16[4,256,256]{2,1,0:T(8,128)(2,1)S(1)}, bf16[4,256,256]{2,1,0:T(8,128)(2,1)S(1)}, u32[]{:S(2)}, u32[]{:S(2)}) collective-permute-start(bf16[4,256,256]{2,1,0:T(8,128)(2,1)S(1)} %all-to-all-done.1), channel_id=1, source_target_pairs={{0,1},{1,0},{2,3},{3,2},{4,5},{5,4},{6,7},{7,6},{8,9},{9,8},{10,11... | collective-permute-start | bytes 1572872 | tf_op jit(solution)/shard_map/ppermute | solution.py:148
  48.4 3.9 %collective-permute-start.3 = (bf16[4,16,16,256]{3,2,1,0:T(8,128)(2,1)S(1)}, bf16[4,16,16,256]{3,2,1,0:T(8,128)(2,1)S(1)}, u32[]{:S(2)}, u32[]{:S(2)}) collective-permute-start(bf16[4,16,16,256]{3,2,1,0:T(8,128)(2,1)S(1)} %get-tuple-element.26), channel_id=1, source_target_pairs={{0,1},{1,0},{2,3},{3,2},{4,5},{5,4},{6,7},{7,6},{8,9},{9,8},{10,11... | collective-permute-start | bytes 1572872 | tf_op jit(solution)/shard_map/ppermute | solution.py:173

commit v4 on v3

--- a/solution.py
+++ b/solution.py
@@ -24,10 +24,12 @@
 
 def feature_rows(ref, x, core, shape, order):
     n_x, _, blk, _ = shape
+    z_order, x_order = order
+    at = x_order[x]
     return jnp.concatenate(
         [
-            ref[pl.ds(pl.multiple_of((z * n_x + x) * 2 * blk + core * blk, blk), blk), :]
-            for z in order
+            ref[pl.ds(pl.multiple_of((z * n_x + at) * 2 * blk + core * blk, blk), blk), :]
+            for z in z_order
         ],
         axis=0,
     )
@@ -134,16 +136,17 @@
     def low(*shape):
         return jax.ShapeDtypeStruct(shape, jnp.bfloat16)
 
-    order = sum_order = from_member(n_z, n_z // 2)
+    order = from_member(n_z, n_z * 11 // 16), from_member(n_x, 0)
+    sum_order = from_member(n_z, n_z // 2), from_member(n_x, n_x // 2)
     to_z = jnp.broadcast_to(memory[0].T, (n_z, blk, rows))
-    along_z = lax.all_to_all(to_z, "z", 0, 0, axis_index_groups=[order])
+    along_z = lax.all_to_all(to_z, "z", 0, 0, axis_index_groups=[order[0]])
     length = jnp.broadcast_to(target_lengths.astype(jnp.float32), (blk, rows))
     tokens = length + lax.ppermute(length, "y", [(y, y ^ 1) for y in range(n_y)])
     along_z, tokens = lax.optimization_barrier((along_z, tokens))
     along_z = along_z.reshape(n_z * blk, rows)
     to_x = jnp.broadcast_to(along_z, (n_x, n_z * blk, rows))
-    own = lax.all_to_all(to_x, X, 0, 0)
-    tokens = tokens + lax.ppermute(tokens, "y", [(y, y ^ 2) for y in range(n_y)])
+    own = lax.all_to_all(to_x, X, 0, 0, axis_index_groups=[order[1]])
+    tokens = tokens + lax.ppermute(tokens, "y", [(y, n_y - 1 - y) for y in range(n_y)])
     own, loss_weight = lax.optimization_barrier((own, float(n_y * t_rows) / tokens))
     other = lax.ppermute(own, "c", swap).reshape(half)
     w_value, query, cot, own_m, key_part = pl.pallas_call(
@@ -180,9 +183,11 @@
         cost_estimate=pl.CostEstimate(flops=540000000, bytes_accessed=5 << 20, transcendentals=0),
     )(core, w_key, w_value, key_grad, value_grad)
     pair = (keep.astype(jnp.float32) + got.astype(jnp.float32)).astype(jnp.bfloat16)
-    parts = lax.all_to_all(pair.reshape(n_x, n_z * blk, rows), X, 0, 0)
+    parts = lax.all_to_all(
+        pair.reshape(n_x, n_z * blk, rows), X, 0, 0, axis_index_groups=[sum_order[1]]
+    )
     row_sum = jnp.sum(parts.astype(jnp.float32), axis=0).astype(jnp.bfloat16)
-    parts = lax.all_to_all(row_sum.reshape(n_z, blk, rows), "z", 0, 0, axis_index_groups=[sum_order])
+    parts = lax.all_to_all(row_sum.reshape(n_z, blk, rows), "z", 0, 0, axis_index_groups=[sum_order[0]])
     own_grad = jnp.sum(parts.astype(jnp.float32), axis=0) * loss_weight
     return context[None, None], own_grad.T[None]
 

time: 84.3 us -> 82.6 us (0.980)
  the two profiles are of different devices: /device:TPU:24 before, /device:TPU:4 now
where the time goes in v4:
time: 82.6 us; the launch traced here: 82.1 us
  starting transfers between devices  33.7 us (41%)
  blocking collectives  30.6 us (37%)
  waiting for transfers between devices  7.65 us (9%)
  Pallas kernels  5.63 us (7%)
  local copies, waits for them, and re-layouts  2.34 us (3%)
  between operations  1.4 us (2%)
  other arithmetic  0.88 us (1%)
    all_to_all x1, blocking collectives, on_device(): lax.all_to_all(row_sum.reshape(n_z, blk, rows), 'z', 0, 0, axis_index_gro...  17.9 us
    all_to_all x1, starting transfers between devices, on_device(): along_z = lax.all_to_all(to_z, 'z', 0, 0, axis_index_groups=[order[0]])  16.2 us
    all_to_all x1, blocking collectives, on_device(): lax.all_to_all(pair.reshape(n_x, n_z * blk, rows), X, 0, 0, axis_index_gr...  12.7 us
    ppermute x1, starting transfers between devices, on_device(): lax.ppermute(tokens, 'y', [(y, n_y - 1 - y) for y in range(n_y)])  4.91 us
    all_to_all x1, starting transfers between devices, on_device(): own = lax.all_to_all(to_x, X, 0, 0, axis_index_groups=[order[1]])  4.8 us
    ppermute x1, starting transfers between devices, on_device(): lax.ppermute(length, 'y', [(y, y ^ 1) for y in range(n_y)])  3.48 us
    pallas_call x1, Pallas kernels, on_device(): pl.pallas_call(functools.partial(main_kernel, order, sum_order), out_shap...  2.96 us
    all_to_all x1, waiting for transfers between devices, on_device(): along_z = lax.all_to_all(to_z, 'z', 0, 0, axis_index_groups=[order[0]])  2.82 us
  transfers between devices with their start and end apart: 6, of which 4 were waited for; matrix products, arithmetic and copies ran while one was open for 0% of the time, Pallas kernels for 3%

profile of v4, /device:TPU:4, one launch (start us, length us, event | category | flops | bytes accessed | tf_op | source)
XLA Modules:
  0.0 82.1 jit_solution(17304379108801054649)
XLA Ops:
  0.6 0.0 copy-start
  0.6 1.5 %broadcast_in_dim.18 = bf16[16,16,256]{2,1,0:T(8,128)(2,1)} broadcast(bf16[16,256]{1,0:T(8,128)(2,1)} %bitcast.30), dimensions={1,2} | broadcast | bytes 139264 | tf_op jit(solution)/shard_map/broadcast_in_dim | solution.py:141
  2.1 16.2 %all-to-all-start = ((bf16[16,16,256]{2,1,0:T(8,128)(2,1)}), bf16[16,16,256]{2,1,0:T(8,128)(2,1)S(1)}, u32[]{:S(2)}, u32[]{:S(2)}) async-start(bf16[16,16,256]{2,1,0:T(8,128)(2,1)} %broadcast_in_dim.18), calls=%async_computation | async-start | bytes 262144 | tf_op jit(solution)/shard_map/all_to_all | solution.py:142
  19.0 3.5 %collective-permute-start = (f32[16,256]{1,0:T(8,128)S(1)}, f32[16,256]{1,0:T(8,128)S(1)}, u32[]{:S(2)}, u32[]{:S(2)}) collective-permute-start(f32[16,256]{1,0:T(8,128)S(1)} %broadcast_in_dim.17.length_ref), channel_id=1, source_target_pairs={{0,4},{4,0},{8,12},{12,8},{1,5},{5,1},{9,13},{13,9},{2,6},{6,2},{1... | collective-permute-start | bytes 49160 | tf_op jit(solution)/shard_map/ppermute | solution.py:144
  22.5 2.1 %collective-permute-done = f32[16,256]{1,0:T(8,128)S(1)} collective-permute-done((f32[16,256]{1,0:T(8,128)S(1)}, f32[16,256]{1,0:T(8,128)S(1)}, u32[]{:S(2)}, u32[]{:S(2)}) %collective-permute-start) | collective-permute-done | bytes 16416 | tf_op jit(solution)/shard_map/ppermute | solution.py:144
  24.6 2.8 %all-to-all-done = bf16[16,16,256]{2,1,0:T(8,128)(2,1)S(1)} async-done(((bf16[16,16,256]{2,1,0:T(8,128)(2,1)}), bf16[16,16,256]{2,1,0:T(8,128)(2,1)S(1)}, u32[]{:S(2)}, u32[]{:S(2)}) %all-to-all-start) | async-done | bytes 131104 | tf_op jit(solution)/shard_map/all_to_all | solution.py:142
  27.4 0.8 broadcast_in_dim.19
  28.2 4.8 %all-to-all-start.1 = ((bf16[4,256,256]{2,1,0:T(8,128)(2,1)}), bf16[4,256,256]{2,1,0:T(8,128)(2,1)S(1)}, u32[]{:S(2)}, u32[]{:S(2)}) async-start(bf16[4,256,256]{2,1,0:T(8,128)(2,1)} %broadcast_in_dim.19), calls=%async_computation.1 | async-start | bytes 1048576 | tf_op jit(solution)/shard_map/all_to_all | solution.py:148
  33.0 4.9 %collective-permute-start.1 = (f32[16,256]{1,0:T(8,128)S(1)}, f32[16,256]{1,0:T(8,128)S(1)}, u32[]{:S(2)}, u32[]{:S(2)}) collective-permute-start(f32[16,256]{1,0:T(8,128)S(1)} %broadcast_add_fusion), channel_id=1, source_target_pairs={{0,12},{4,8},{8,4},{12,0},{1,13},{5,9},{9,5},{13,1},{2,14},{6,10},... | collective-permute-start | bytes 49160 | tf_op jit(solution)/shard_map/ppermute | solution.py:149
  38.0 1.9 %collective-permute-done.1 = f32[16,256]{1,0:T(8,128)S(1)} collective-permute-done((f32[16,256]{1,0:T(8,128)S(1)}, f32[16,256]{1,0:T(8,128)S(1)}, u32[]{:S(2)}, u32[]{:S(2)}) %collective-permute-start.1) | collective-permute-done | bytes 16416 | tf_op jit(solution)/shard_map/ppermute | solution.py:149
  39.9 0.0 all-to-all-done.1
  39.9 1.9 %collective-permute-start.2 = (bf16[4,256,256]{2,1,0:T(8,128)(2,1)S(1)}, bf16[4,256,256]{2,1,0:T(8,128)(2,1)S(1)}, u32[]{:S(2)}, u32[]{:S(2)}) collective-permute-start(bf16[4,256,256]{2,1,0:T(8,128)(2,1)S(1)} %all-to-all-done.1), channel_id=1, source_target_pairs={{0,1},{1,0},{2,3},{3,2},{4,5},{5,4},{6,7},{7,6},{8,9},{9,8},{10,11... | collective-permute-start | bytes 1572872 | tf_op jit(solution)/shard_map/ppermute | solution.py:151
  41.8 0.0 copy-done
  41.8 1.9 %shard_map.77 = (bf16[2048,512]{1,0:T(8,128)(2,1)S(1)}, bf16[256,512]{1,0:T(8,128)(2,1)S(1)}, bf16[256,512]{1,0:T(8,128)(2,1)S(1)}, bf16[256,1024]{1,0:T(8,128)(2,1)S(1)}, f32[256,512]{1,0:T(8,128)S(1)}) custom-call(s32[1]{0:T(128)} %bitcast.core_ref, bf16[4,16,16,256]{3,2,1,0:T(8,128)(2,1)S(1)} %bitcast.22, bf16[2048,512]{1,0:T(8,128)(2,1)S(1)} %bitcast.19, ...), custom_call_target="tpu_custom_call" | custom-call | flops 270000000 | bytes 8388608 | tf_op jit(solution)/shard_map/pallas_call | solution.py:152
  43.8 0.0 collective-permute-done.2
  43.8 3.0 %shard_map.78 = (bf16[256,512]{1,0:T(8,128)(2,1)}, bf16[4,16,16,256]{3,2,1,0:T(8,128)(2,1)S(1)}, bf16[256,512]{1,0:T(8,128)(2,1)S(1)}, bf16[256,512]{1,0:T(8,128)(2,1)S(1)}) custom-call(s32[1]{0:T(128)} %bitcast.core_ref, f32[16,256]{1,0:T(8,128)S(1)} %broadcast_in_dim.17.length_ref, bf16[4,16,16,256]{3,2,1,0:T(8,128)(2,1)S(1)} %bitcast.23, ...), custom_call_target="tpu_custom_call" | custom-call | flops 1700000000 | bytes 8388608 | tf_op jit(solution)/shard_map/pallas_call | solution.py:164
  46.8 2.4 %collective-permute-start.3 = (bf16[4,16,16,256]{3,2,1,0:T(8,128)(2,1)S(1)}, bf16[4,16,16,256]{3,2,1,0:T(8,128)(2,1)S(1)}, u32[]{:S(2)}, u32[]{:S(2)}) collective-permute-start(bf16[4,16,16,256]{3,2,1,0:T(8,128)(2,1)S(1)} %get-tuple-element.26), channel_id=1, source_target_pairs={{0,1},{1,0},{2,3},{3,2},{4,5},{5,4},{6,7},{7,6},{8,9},{9,8},{10,11... | collective-permute-start | bytes 1572872 | tf_op jit(solution)/shard_map/ppermute | solution.py:176
  49.2 0.7 shard_map.79
  49.9 0.8 collective-permute-done.3
  50.7 0.2 add_convert_fusion
  50.9 12.7 %all_to_all.20 = bf16[4,256,256]{2,1,0:T(8,128)(2,1)S(1)} all-to-all(bf16[4,256,256]{2,1,0:T(8,128)(2,1)S(1)} %bitcast.24), channel_id=1, replica_groups={{16,18,0,2},{17,19,1,3},{20,22,4,6},{21,23,5,7},{24,26,8,10},{25,27,9,1..., dimensions={0} | all-to-all | bytes 1048576 | tf_op jit(solution)/shard_map/all_to_all | solution.py:186
  63.6 0.1 reduce_sum.21
  63.6 17.9 %all_to_all.21 = bf16[16,16,256]{2,1,0:T(8,128)(2,1)S(1)} all-to-all(bf16[16,16,256]{2,1,0:T(8,128)(2,1)S(1)} %bitcast.27), channel_id=1, replica_groups={{256,288,320,352,384,416,448,480,0,32,64,96,128,160,192,224},{257,289,3..., dimensions={0} | all-to-all | bytes 262144 | tf_op jit(solution)/shard_map/all_to_all | solution.py:190
  81.5 0.6 multiply_bitcast_fusion
  (4 shorter events, 0.0 us)
Async XLA Ops:
  0.6 41.2 %copy-start = (bf16[1,2048,512]{2,1,0:T(8,128)(2,1)S(1)}, bf16[1,2048,512]{2,1,0:T(8,128)(2,1)}, u32[]{:S(2)}) copy-start(bf16[1,2048,512]{2,1,0:T(8,128)(2,1)} %param.7) | copy-start | bytes 6291460
  2.1 25.3 %all-to-all-start = ((bf16[16,16,256]{2,1,0:T(8,128)(2,1)}), bf16[16,16,256]{2,1,0:T(8,128)(2,1)S(1)}, u32[]{:S(2)}, u32[]{:S(2)}) async-start(bf16[16,16,256]{2,1,0:T(8,128)(2,1)} %broadcast_in_dim.18), calls=%async_computation | async-start | bytes 262144 | tf_op jit(solution)/shard_map/all_to_all | solution.py:142
  19.0 5.6 %collective-permute-start = (f32[16,256]{1,0:T(8,128)S(1)}, f32[16,256]{1,0:T(8,128)S(1)}, u32[]{:S(2)}, u32[]{:S(2)}) collective-permute-start(f32[16,256]{1,0:T(8,128)S(1)} %broadcast_in_dim.17.length_ref), channel_id=1, source_target_pairs={{0,4},{4,0},{8,12},{12,8},{1,5},{5,1},{9,13},{13,9},{2,6},{6,2},{1... | collective-permute-start | bytes 49160 | tf_op jit(solution)/shard_map/ppermute | solution.py:144
  28.2 11.6 %all-to-all-start.1 = ((bf16[4,256,256]{2,1,0:T(8,128)(2,1)}), bf16[4,256,256]{2,1,0:T(8,128)(2,1)S(1)}, u32[]{:S(2)}, u32[]{:S(2)}) async-start(bf16[4,256,256]{2,1,0:T(8,128)(2,1)} %broadcast_in_dim.19), calls=%async_computation.1 | async-start | bytes 1048576 | tf_op jit(solution)/shard_map/all_to_all | solution.py:148
  33.0 6.8 %collective-permute-start.1 = (f32[16,256]{1,0:T(8,128)S(1)}, f32[16,256]{1,0:T(8,128)S(1)}, u32[]{:S(2)}, u32[]{:S(2)}) collective-permute-start(f32[16,256]{1,0:T(8,128)S(1)} %broadcast_add_fusion), channel_id=1, source_target_pairs={{0,12},{4,8},{8,4},{12,0},{1,13},{5,9},{9,5},{13,1},{2,14},{6,10},... | collective-permute-start | bytes 49160 | tf_op jit(solution)/shard_map/ppermute | solution.py:149
  39.9 3.9 %collective-permute-start.2 = (bf16[4,256,256]{2,1,0:T(8,128)(2,1)S(1)}, bf16[4,256,256]{2,1,0:T(8,128)(2,1)S(1)}, u32[]{:S(2)}, u32[]{:S(2)}) collective-permute-start(bf16[4,256,256]{2,1,0:T(8,128)(2,1)S(1)} %all-to-all-done.1), channel_id=1, source_target_pairs={{0,1},{1,0},{2,3},{3,2},{4,5},{5,4},{6,7},{7,6},{8,9},{9,8},{10,11... | collective-permute-start | bytes 1572872 | tf_op jit(solution)/shard_map/ppermute | solution.py:151
  46.8 3.9 %collective-permute-start.3 = (bf16[4,16,16,256]{3,2,1,0:T(8,128)(2,1)S(1)}, bf16[4,16,16,256]{3,2,1,0:T(8,128)(2,1)S(1)}, u32[]{:S(2)}, u32[]{:S(2)}) collective-permute-start(bf16[4,16,16,256]{3,2,1,0:T(8,128)(2,1)S(1)} %get-tuple-element.26), channel_id=1, source_target_pairs={{0,1},{1,0},{2,3},{3,2},{4,5},{5,4},{6,7},{7,6},{8,9},{9,8},{10,11... | collective-permute-start | bytes 1572872 | tf_op jit(solution)/shard_map/ppermute | solution.py:176

commit v5 on v4

--- a/solution.py
+++ b/solution.py
@@ -60,7 +60,7 @@
 
 def main_kernel(
     order, sum_order, core_ref, length_ref, other_ref, own_m_ref, key_part_ref, wk_ref, wv_ref, q_ref, cot_ref,
-    context_hbm, send_ref, kg_ref, vg_ref, context_ref, sem,
+    send_ref, kg_ref, vg_ref, probs_ref, values_ref,
 ):
     n_x, n_z, blk, rows = other_ref.shape
     core = core_ref[0]
@@ -85,11 +85,9 @@
         weights = jnp.exp(scores - jnp.max(scores, axis=0, keepdims=True))
         probs = weights * (1.0 / jnp.sum(weights, axis=0, keepdims=True))
         probs_low = probs.astype(jnp.bfloat16)
-        context = dot(probs_low, values[:, cols], TN)
-        context_ref[:, cols] = jnp.where(valid, context, 0.0).astype(jnp.bfloat16)
+        probs_ref[:, len(kept) * t_rows:(len(kept) + 1) * t_rows] = probs_low
         kept.append((probs, probs_low))
-    out = pltpu.make_async_copy(context_ref, context_hbm, sem)
-    out.start()
+    values_ref[...] = values
     for cols, (probs, probs_low) in zip(heads, kept):
         cot = jnp.where(valid, cot_ref[:, cols].astype(jnp.float32), 0.0).astype(jnp.bfloat16)
         vg_ref[:, cols] = dot(probs_low, cot).astype(jnp.bfloat16)
@@ -98,7 +96,6 @@
         score_grad = (probs * (prob_grad - row_dot) * scale).astype(jnp.bfloat16)
         kg_ref[:, cols] = dot(score_grad, q_ref[:, cols]).astype(jnp.bfloat16)
     half_grad(sum_order, 1 - core, wk_ref, wv_ref, kg_ref, vg_ref, send_ref)
-    out.wait()
 
 
 def half_grad(order, core, wk_ref, wv_ref, kg_ref, vg_ref, out_ref):
@@ -110,8 +107,23 @@
         out_ref[x] = grad.astype(jnp.bfloat16).reshape(n_z, blk, rows)
 
 
-def keep_kernel(order, core_ref, wk_ref, wv_ref, kg_ref, vg_ref, keep_ref):
+def keep_kernel(
+    order, core_ref, length_ref, wk_ref, wv_ref, kg_ref, vg_ref, probs_ref, values_ref,
+    context_hbm, keep_ref, context_ref, sem,
+):
+    t_rows, width = context_ref.shape
+    row = lax.broadcasted_iota(jnp.int32, (t_rows, HEAD_DIM), 0)
+    valid = row.astype(jnp.float32) < length_ref[0:1, 0:1]
+    for h in range(0, width, HEAD_DIM):
+        cols = slice(h, h + HEAD_DIM)
+        head = h // HEAD_DIM
+        probs_low = probs_ref[:, head * t_rows:(head + 1) * t_rows]
+        context = dot(probs_low, values_ref[:, cols], TN)
+        context_ref[:, cols] = jnp.where(valid, context, 0.0).astype(jnp.bfloat16)
+    out = pltpu.make_async_copy(context_ref, context_hbm, sem)
+    out.start()
     half_grad(order, core_ref[0], wk_ref, wv_ref, kg_ref, vg_ref, keep_ref)
+    out.wait()
 
 
 def on_device(memory, key_weight, value_weight, queries, cotangent, target_lengths):
@@ -137,7 +149,7 @@
         return jax.ShapeDtypeStruct(shape, jnp.bfloat16)
 
     order = from_member(n_z, n_z * 11 // 16), from_member(n_x, 0)
-    sum_order = from_member(n_z, n_z // 2), from_member(n_x, n_x // 2)
+    sum_order = from_member(n_z, n_z // 2 + 1), from_member(n_x, n_x // 2)
     to_z = jnp.broadcast_to(memory[0].T, (n_z, blk, rows))
     along_z = lax.all_to_all(to_z, "z", 0, 0, axis_index_groups=[order[0]])
     length = jnp.broadcast_to(target_lengths.astype(jnp.float32), (blk, rows))
@@ -161,27 +173,25 @@
         compiler_params=params,
         cost_estimate=pl.CostEstimate(flops=270000000, bytes_accessed=8 << 20, transcendentals=0),
     )(core, own.reshape(half), w_key, w_value, query, cot)
-    context, send, key_grad, value_grad = pl.pallas_call(
+    wide = low(rows, width // HEAD_DIM * t_rows)
+    send, key_grad, value_grad, probs, values = pl.pallas_call(
         functools.partial(main_kernel, order, sum_order),
-        out_shape=(low(t_rows, width), low(*half), low(rows, width), low(rows, width)),
+        out_shape=(low(*half), low(rows, width), low(rows, width), wide, low(rows, width)),
         in_specs=[smem] + [vmem] * 8,
-        out_specs=(hbm, vmem, vmem, vmem),
-        scratch_shapes=[
-            pltpu.VMEM((t_rows, width), jnp.bfloat16),
-            pltpu.SemaphoreType.DMA,
-        ],
+        out_specs=(vmem,) * 5,
         compiler_params=params,
-        cost_estimate=pl.CostEstimate(flops=1700000000, bytes_accessed=8 << 20, transcendentals=1 << 17),
+        cost_estimate=pl.CostEstimate(flops=1600000000, bytes_accessed=8 << 20, transcendentals=1 << 17),
     )(core, length, other, own_m, key_part, w_key, w_value, query, cot)
     got = lax.ppermute(send, "c", swap)
-    keep = pl.pallas_call(
+    context, keep = pl.pallas_call(
         functools.partial(keep_kernel, sum_order),
-        out_shape=low(*half),
-        in_specs=[smem] + [vmem] * 4,
-        out_specs=vmem,
+        out_shape=(low(t_rows, width), low(*half)),
+        in_specs=[smem] + [vmem] * 7,
+        out_specs=(hbm, vmem),
+        scratch_shapes=[pltpu.VMEM((t_rows, width), jnp.bfloat16), pltpu.SemaphoreType.DMA],
         compiler_params=params,
-        cost_estimate=pl.CostEstimate(flops=540000000, bytes_accessed=5 << 20, transcendentals=0),
-    )(core, w_key, w_value, key_grad, value_grad)
+        cost_estimate=pl.CostEstimate(flops=600000000, bytes_accessed=5 << 20, transcendentals=0),
+    )(core, length, w_key, w_value, key_grad, value_grad, probs, values)
     pair = (keep.astype(jnp.float32) + got.astype(jnp.float32)).astype(jnp.bfloat16)
     parts = lax.all_to_all(
         pair.reshape(n_x, n_z * blk, rows), X, 0, 0, axis_index_groups=[sum_order[1]]

time: 82.6 us -> 82 us (level)
  the two profiles are of different devices: /device:TPU:4 before, /device:TPU:24 now
where the time goes in v5:
time: 82 us; the launch traced here: 81.6 us
  blocking collectives  29.6 us (36%)
  starting transfers between devices  29.5 us (36%)
  waiting for transfers between devices  12.2 us (15%)
  Pallas kernels  5.63 us (7%)
  local copies, waits for them, and re-layouts  2.34 us (3%)
  between operations  1.39 us (2%)
  other arithmetic  0.88 us (1%)
    all_to_all x1, blocking collectives, on_device(): lax.all_to_all(row_sum.reshape(n_z, blk, rows), 'z', 0, 0, axis_index_gro...  17.9 us
    all_to_all x1, starting transfers between devices, on_device(): along_z = lax.all_to_all(to_z, 'z', 0, 0, axis_index_groups=[order[0]])  16.2 us
    all_to_all x1, blocking collectives, on_device(): lax.all_to_all(pair.reshape(n_x, n_z * blk, rows), X, 0, 0, axis_index_gr...  11.8 us
    ppermute x1, waiting for transfers between devices, on_device(): lax.ppermute(tokens, 'y', [(y, n_y - 1 - y) for y in range(n_y)])  4.7 us
    all_to_all x1, starting transfers between devices, on_device(): own = lax.all_to_all(to_x, X, 0, 0, axis_index_groups=[order[1]])  4.29 us
    ppermute x1, waiting for transfers between devices, on_device(): lax.ppermute(length, 'y', [(y, y ^ 1) for y in range(n_y)])  2.97 us
    all_to_all x1, waiting for transfers between devices, on_device(): along_z = lax.all_to_all(to_z, 'z', 0, 0, axis_index_groups=[order[0]])  2.82 us
    ppermute x1, starting transfers between devices, on_device(): lax.ppermute(length, 'y', [(y, y ^ 1) for y in range(n_y)])  2.65 us
  transfers between devices with their start and end apart: 6, of which 5 were waited for; matrix products, arithmetic and copies ran while one was open for 0% of the time, Pallas kernels for 4%

profile of v5, /device:TPU:24, one launch (start us, length us, event | category | flops | bytes accessed | tf_op | source)
XLA Modules:
  0.0 81.6 jit_solution(9313631507762339562)
XLA Ops:
  0.6 0.0 copy-start
  0.6 1.5 %broadcast_in_dim.18 = bf16[16,16,256]{2,1,0:T(8,128)(2,1)} broadcast(bf16[16,256]{1,0:T(8,128)(2,1)} %bitcast.30), dimensions={1,2} | broadcast | bytes 139264 | tf_op jit(solution)/shard_map/broadcast_in_dim | solution.py:153
  2.1 16.2 %all-to-all-start = ((bf16[16,16,256]{2,1,0:T(8,128)(2,1)}), bf16[16,16,256]{2,1,0:T(8,128)(2,1)S(1)}, u32[]{:S(2)}, u32[]{:S(2)}) async-start(bf16[16,16,256]{2,1,0:T(8,128)(2,1)} %broadcast_in_dim.18), calls=%async_computation | async-start | bytes 262144 | tf_op jit(solution)/shard_map/all_to_all | solution.py:154
  19.0 2.7 %collective-permute-start = (f32[16,256]{1,0:T(8,128)S(1)}, f32[16,256]{1,0:T(8,128)S(1)}, u32[]{:S(2)}, u32[]{:S(2)}) collective-permute-start(f32[16,256]{1,0:T(8,128)S(1)} %broadcast_in_dim.17.length_ref), channel_id=1, source_target_pairs={{0,4},{4,0},{8,12},{12,8},{1,5},{5,1},{9,13},{13,9},{2,6},{6,2},{1... | collective-permute-start | bytes 49160 | tf_op jit(solution)/shard_map/ppermute | solution.py:156
  21.6 3.0 %collective-permute-done = f32[16,256]{1,0:T(8,128)S(1)} collective-permute-done((f32[16,256]{1,0:T(8,128)S(1)}, f32[16,256]{1,0:T(8,128)S(1)}, u32[]{:S(2)}, u32[]{:S(2)}) %collective-permute-start) | collective-permute-done | bytes 16416 | tf_op jit(solution)/shard_map/ppermute | solution.py:156
  24.6 2.8 %all-to-all-done = bf16[16,16,256]{2,1,0:T(8,128)(2,1)S(1)} async-done(((bf16[16,16,256]{2,1,0:T(8,128)(2,1)}), bf16[16,16,256]{2,1,0:T(8,128)(2,1)S(1)}, u32[]{:S(2)}, u32[]{:S(2)}) %all-to-all-start) | async-done | bytes 131104 | tf_op jit(solution)/shard_map/all_to_all | solution.py:154
  27.4 0.8 %broadcast_in_dim.19 = bf16[4,256,256]{2,1,0:T(8,128)(2,1)} broadcast(bf16[256,256]{1,0:T(8,128)(2,1)S(1)} %bitcast.26), dimensions={1,2} | broadcast | bytes 655360 | tf_op jit(solution)/shard_map/broadcast_in_dim | solution.py:159
  28.2 4.3 %all-to-all-start.1 = ((bf16[4,256,256]{2,1,0:T(8,128)(2,1)}), bf16[4,256,256]{2,1,0:T(8,128)(2,1)S(1)}, u32[]{:S(2)}, u32[]{:S(2)}) async-start(bf16[4,256,256]{2,1,0:T(8,128)(2,1)} %broadcast_in_dim.19), calls=%async_computation.1 | async-start | bytes 1048576 | tf_op jit(solution)/shard_map/all_to_all | solution.py:160
  32.5 2.1 %collective-permute-start.1 = (f32[16,256]{1,0:T(8,128)S(1)}, f32[16,256]{1,0:T(8,128)S(1)}, u32[]{:S(2)}, u32[]{:S(2)}) collective-permute-start(f32[16,256]{1,0:T(8,128)S(1)} %broadcast_add_fusion), channel_id=1, source_target_pairs={{0,12},{4,8},{8,4},{12,0},{1,13},{5,9},{9,5},{13,1},{2,14},{6,10},... | collective-permute-start | bytes 49160 | tf_op jit(solution)/shard_map/ppermute | solution.py:161
  34.7 4.7 %collective-permute-done.1 = f32[16,256]{1,0:T(8,128)S(1)} collective-permute-done((f32[16,256]{1,0:T(8,128)S(1)}, f32[16,256]{1,0:T(8,128)S(1)}, u32[]{:S(2)}, u32[]{:S(2)}) %collective-permute-start.1) | collective-permute-done | bytes 16416 | tf_op jit(solution)/shard_map/ppermute | solution.py:161
  39.4 1.5 %all-to-all-done.1 = bf16[4,256,256]{2,1,0:T(8,128)(2,1)S(1)} async-done(((bf16[4,256,256]{2,1,0:T(8,128)(2,1)}), bf16[4,256,256]{2,1,0:T(8,128)(2,1)S(1)}, u32[]{:S(2)}, u32[]{:S(2)}) %all-to-all-start.1) | async-done | bytes 524320 | tf_op jit(solution)/shard_map/all_to_all | solution.py:160
  40.9 1.9 %collective-permute-start.2 = (bf16[4,256,256]{2,1,0:T(8,128)(2,1)S(1)}, bf16[4,256,256]{2,1,0:T(8,128)(2,1)S(1)}, u32[]{:S(2)}, u32[]{:S(2)}) collective-permute-start(bf16[4,256,256]{2,1,0:T(8,128)(2,1)S(1)} %all-to-all-done.1), channel_id=1, source_target_pairs={{0,1},{1,0},{2,3},{3,2},{4,5},{5,4},{6,7},{7,6},{8,9},{9,8},{10,11... | collective-permute-start | bytes 1572872 | tf_op jit(solution)/shard_map/ppermute | solution.py:163
  42.8 0.0 copy-done
  42.8 1.9 %shard_map.77 = (bf16[2048,512]{1,0:T(8,128)(2,1)S(1)}, bf16[256,512]{1,0:T(8,128)(2,1)S(1)}, bf16[256,512]{1,0:T(8,128)(2,1)S(1)}, bf16[256,1024]{1,0:T(8,128)(2,1)S(1)}, f32[256,512]{1,0:T(8,128)S(1)}) custom-call(s32[1]{0:T(128)} %bitcast.core_ref, bf16[4,16,16,256]{3,2,1,0:T(8,128)(2,1)S(1)} %bitcast.22, bf16[2048,512]{1,0:T(8,128)(2,1)S(1)} %bitcast.19, ...), custom_call_target="tpu_custom_call" | custom-call | flops 270000000 | bytes 8388608 | tf_op jit(solution)/shard_map/pallas_call | solution.py:164
  44.8 0.0 collective-permute-done.2
  44.8 2.3 %shard_map.78 = (bf16[4,16,16,256]{3,2,1,0:T(8,128)(2,1)S(1)}, bf16[256,512]{1,0:T(8,128)(2,1)S(1)}, bf16[256,512]{1,0:T(8,128)(2,1)S(1)}, bf16[256,512]{1,0:T(8,128)(2,1)S(1)}, bf16[256,512]{1,0:T(8,128)(2,1)S(1)}) custom-call(s32[1]{0:T(128)} %bitcast.core_ref, f32[16,256]{1,0:T(8,128)S(1)} %broadcast_in_dim.17.length_ref, ...), custom_call_target="tpu_custom_call" | custom-call | flops 1600000000 | bytes 8388608 | tf_op jit(solution)/shard_map/pallas_call | solution.py:177
  47.1 2.4 %collective-permute-start.3 = (bf16[4,16,16,256]{3,2,1,0:T(8,128)(2,1)S(1)}, bf16[4,16,16,256]{3,2,1,0:T(8,128)(2,1)S(1)}, u32[]{:S(2)}, u32[]{:S(2)}) collective-permute-start(bf16[4,16,16,256]{3,2,1,0:T(8,128)(2,1)S(1)} %get-tuple-element.32), channel_id=1, source_target_pairs={{0,1},{1,0},{2,3},{3,2},{4,5},{5,4},{6,7},{7,6},{8,9},{9,8},{10,11... | collective-permute-start | bytes 1572872 | tf_op jit(solution)/shard_map/ppermute | solution.py:185
  49.5 1.4 %shard_map.79 = (bf16[256,512]{1,0:T(8,128)(2,1)}, bf16[4,16,16,256]{3,2,1,0:T(8,128)(2,1)S(1)}) custom-call(s32[1]{0:T(128)} %bitcast.core_ref, f32[16,256]{1,0:T(8,128)S(1)} %broadcast_in_dim.17.length_ref, bf16[2048,512]{1,0:T(8,128)(2,1)S(1)} %bitcast.21, bf16[2048,512]{1,0:T(8,128)(2,1)S(1)} %get-tuple-element.21.wv_ref, ...), custom_call_target="tpu_custom_call" | custom-call | flops 600000000 | bytes 5242880 | tf_op jit(solution)/shard_map/pallas_call | solution.py:186
  50.9 0.2 collective-permute-done.3
  51.1 0.2 add_convert_fusion
  51.2 11.8 %all_to_all.20 = bf16[4,256,256]{2,1,0:T(8,128)(2,1)S(1)} all-to-all(bf16[4,256,256]{2,1,0:T(8,128)(2,1)S(1)} %bitcast.24), channel_id=1, replica_groups={{16,18,0,2},{17,19,1,3},{20,22,4,6},{21,23,5,7},{24,26,8,10},{25,27,9,1..., dimensions={0} | all-to-all | bytes 1048576 | tf_op jit(solution)/shard_map/all_to_all | solution.py:196
  63.0 0.1 reduce_sum.21
  63.1 17.9 %all_to_all.21 = bf16[16,16,256]{2,1,0:T(8,128)(2,1)S(1)} all-to-all(bf16[16,16,256]{2,1,0:T(8,128)(2,1)S(1)} %bitcast.27), channel_id=1, replica_groups={{288,320,352,384,416,448,480,0,32,64,96,128,160,192,224,256},{289,321,3..., dimensions={0} | all-to-all | bytes 262144 | tf_op jit(solution)/shard_map/all_to_all | solution.py:200
  81.0 0.6 multiply_bitcast_fusion
  (4 shorter events, 0.0 us)
Async XLA Ops:
  0.6 42.2 %copy-start = (bf16[1,2048,512]{2,1,0:T(8,128)(2,1)S(1)}, bf16[1,2048,512]{2,1,0:T(8,128)(2,1)}, u32[]{:S(2)}) copy-start(bf16[1,2048,512]{2,1,0:T(8,128)(2,1)} %param.7) | copy-start | bytes 6291460
  2.1 25.3 %all-to-all-start = ((bf16[16,16,256]{2,1,0:T(8,128)(2,1)}), bf16[16,16,256]{2,1,0:T(8,128)(2,1)S(1)}, u32[]{:S(2)}, u32[]{:S(2)}) async-start(bf16[16,16,256]{2,1,0:T(8,128)(2,1)} %broadcast_in_dim.18), calls=%async_computation | async-start | bytes 262144 | tf_op jit(solution)/shard_map/all_to_all | solution.py:154
  19.0 5.6 %collective-permute-start = (f32[16,256]{1,0:T(8,128)S(1)}, f32[16,256]{1,0:T(8,128)S(1)}, u32[]{:S(2)}, u32[]{:S(2)}) collective-permute-start(f32[16,256]{1,0:T(8,128)S(1)} %broadcast_in_dim.17.length_ref), channel_id=1, source_target_pairs={{0,4},{4,0},{8,12},{12,8},{1,5},{5,1},{9,13},{13,9},{2,6},{6,2},{1... | collective-permute-start | bytes 49160 | tf_op jit(solution)/shard_map/ppermute | solution.py:156
  28.2 12.6 %all-to-all-start.1 = ((bf16[4,256,256]{2,1,0:T(8,128)(2,1)}), bf16[4,256,256]{2,1,0:T(8,128)(2,1)S(1)}, u32[]{:S(2)}, u32[]{:S(2)}) async-start(bf16[4,256,256]{2,1,0:T(8,128)(2,1)} %broadcast_in_dim.19), calls=%async_computation.1 | async-start | bytes 1048576 | tf_op jit(solution)/shard_map/all_to_all | solution.py:160
  32.5 6.8 %collective-permute-start.1 = (f32[16,256]{1,0:T(8,128)S(1)}, f32[16,256]{1,0:T(8,128)S(1)}, u32[]{:S(2)}, u32[]{:S(2)}) collective-permute-start(f32[16,256]{1,0:T(8,128)S(1)} %broadcast_add_fusion), channel_id=1, source_target_pairs={{0,12},{4,8},{8,4},{12,0},{1,13},{5,9},{9,5},{13,1},{2,14},{6,10},... | collective-permute-start | bytes 49160 | tf_op jit(solution)/shard_map/ppermute | solution.py:161
  40.9 3.9 %collective-permute-start.2 = (bf16[4,256,256]{2,1,0:T(8,128)(2,1)S(1)}, bf16[4,256,256]{2,1,0:T(8,128)(2,1)S(1)}, u32[]{:S(2)}, u32[]{:S(2)}) collective-permute-start(bf16[4,256,256]{2,1,0:T(8,128)(2,1)S(1)} %all-to-all-done.1), channel_id=1, source_target_pairs={{0,1},{1,0},{2,3},{3,2},{4,5},{5,4},{6,7},{7,6},{8,9},{9,8},{10,11... | collective-permute-start | bytes 1572872 | tf_op jit(solution)/shard_map/ppermute | solution.py:163
  47.1 3.9 %collective-permute-start.3 = (bf16[4,16,16,256]{3,2,1,0:T(8,128)(2,1)S(1)}, bf16[4,16,16,256]{3,2,1,0:T(8,128)(2,1)S(1)}, u32[]{:S(2)}, u32[]{:S(2)}) collective-permute-start(bf16[4,16,16,256]{3,2,1,0:T(8,128)(2,1)S(1)} %get-tuple-element.32), channel_id=1, source_target_pairs={{0,1},{1,0},{2,3},{3,2},{4,5},{5,4},{6,7},{7,6},{8,9},{9,8},{10,11... | collective-permute-start | bytes 1572872 | tf_op jit(solution)/shard_map/ppermute | solution.py:185
